TPU v7x, 32 devices: a whole 2x2x4 slice. The times are simulated.
32 devices in a mesh: sub: 8 (over y, x, core), reg: 4 (over z).
Axes of the slice: x: 2, y: 2, z: 4, core: 2. Of those that a mesh axis runs over, the one named last changes fastest.
Arguments:
- right_side: float32 [8, 4, 1280, 16], P('sub', 'reg'), may hold values from -6 to 6
- tiles: bfloat16 [8, 4, 80, 128, 128], P('sub', 'reg'), may hold values from -1 to 5
- tile_list: int32 [8, 4, 80, 2], P('sub', 'reg'), may hold values from 0 to 9, as said below
- weights: float32 [8, 4, 1280], P('sub', 'reg'), may hold values from 0.15 to 0.35
- face_map: int32 [8, 4, 6], P('sub', 'reg'), may hold values from 0 to 9, as said below
- matching: int32 [8, 4, 6, 128], P('sub', 'reg'), may hold values from 0 to 127, each once within a row
- coarse_basis: bfloat16 [8, 4, 1280, 128], P('sub', 'reg'), may hold values from -0.15625 to 0.15625
- coarse_map: int32 [8, 4, 128], P('sub', 'reg'), may hold values from 0 to 511, as said below
- coarse_inverse: float32 [4, 512, 512], P('reg', 'sub'), may hold values from -1 to 2, as said below
Outputs:
- solution: bfloat16 [8, 4, 1280, 16], P('sub', 'reg')
- residual: bfloat16 [8, 4, 1280, 16], P('sub', 'reg')
Inputs may be any that keep to these rules, and one draw needn't show every extreme that they name: `tile_list`: entries 0 to 9 of each subdomain's list are (b, b) for b in order; the other 70 entries are distinct off-diagonal block pairs. `face_map`: the six blocks of a subdomain are distinct. `coarse_map`: A subdomain's 128 numbers are distinct, and within a subregion every number is named by exactly two subdomains. `coarse_inverse`: symmetric in its last two dimensions.
All inputs are finite; a program needn't handle non-finite values.
Results may differ from a plain program's by a relative error of at most 0.0075.
Values may be sent and summed in bfloat16 or wider, within the bound.
No kernel may reach another device: no remote copies, remote signals or barrier semaphores. Data moves between devices by JAX's collectives and lax.ppermute only.
A program may use at most 64 MiB of HBM per device.

v0:
```python
import jax
import jax.numpy as jnp
from jax import lax
from jax.sharding import PartitionSpec as P

SWEEPS = 3


def from_behind(shard, axis, by):
    peers = lax.axis_size(axis)
    return lax.ppermute(shard, axis, [(i, (i + by) % peers) for i in range(peers)])


def body(
    right_side,
    tiles,
    tile_list,
    weights,
    face_map,
    matching,
    coarse_basis,
    coarse_map,
    coarse_inverse,
):
    order = right_side.shape[2]
    rights = right_side.shape[3]
    tile = tiles.shape[3]
    blocks = order // tile
    target = right_side[0, 0]
    tile_block = tiles[0, 0]
    listing = tile_list[0, 0]
    scaling = weights[0, 0][:, None]
    faces_here = face_map[0, 0]
    matched = matching[0, 0]
    basis = coarse_basis[0, 0]
    own_map = coarse_map[0, 0]
    own_count = own_map.shape[0]
    inverse_rows = coarse_inverse[0]
    held_rows = inverse_rows.shape[0]
    block_ids = jnp.arange(blocks, dtype=jnp.int32)
    row_table = (listing[:, 0][None, :] == block_ids[:, None]).astype(jnp.float32)
    face_table = (faces_here[None, :] == block_ids[:, None]).astype(jnp.float32)
    stride = max(lax.axis_size("reg") // 4, 1)
    every_ids = lax.all_gather(own_map, "sub", axis=0, tiled=True)
    outgoing_part = jnp.take(inverse_rows, every_ids, axis=1).reshape(
        held_rows, lax.axis_size("sub"), own_count
    )
    received_part = lax.all_to_all(outgoing_part, "sub", split_axis=1, concat_axis=0, tiled=True)
    own_columns = received_part.reshape(held_rows * lax.axis_size("sub"), own_count)
    own_block = jnp.transpose(jnp.take(own_columns, every_ids, axis=0))
    solution = jnp.zeros_like(target)
    residual = target
    for sweep in range(SWEEPS):
        low = residual.astype(jnp.bfloat16)
        local_coarse = jnp.einsum("mn,mr->nr", basis, low, preferred_element_type=jnp.float32)
        own_solution = jnp.dot(
            own_block,
            lax.all_gather(local_coarse, "sub", axis=0, tiled=True),
            precision=lax.Precision.HIGHEST,
            preferred_element_type=jnp.float32,
        )
        own_values = own_solution.astype(jnp.bfloat16)
        correction = jnp.dot(basis, own_values, preferred_element_type=jnp.float32)
        solution = solution + (scaling * residual + correction)
        operator_low = solution.astype(jnp.bfloat16).reshape(blocks, tile, rights)
        picked = jnp.take(operator_low, listing[:, 1], axis=0)
        products = jnp.einsum(
            "tij,tjr->tir", tile_block, picked, preferred_element_type=jnp.float32
        )
        local = jnp.einsum("bt,tir->bir", row_table, products, precision=lax.Precision.HIGHEST)
        stacked = solution.reshape(blocks, tile, rights)
        outgoing = jnp.take(stacked, faces_here, axis=0)
        arrived = []
        for face, offset in ((0, 1), (1, -1), (2, stride), (3, -stride)):
            arrived.append(from_behind(outgoing[face ^ 1], "reg", offset))
        for face, offset in ((4, 1), (5, -1)):
            arrived.append(from_behind(outgoing[face ^ 1], "sub", offset))
        received = jnp.stack(arrived)
        permuted = jnp.take_along_axis(received, matched[:, :, None], axis=1)
        coupling = jnp.einsum("bk,kir->bir", face_table, permuted, precision=lax.Precision.HIGHEST)
        residual = target - (local - 0.5 * coupling).reshape(order, rights)
    shape = (1, 1, order, rights)
    return (
        solution.astype(jnp.bfloat16).reshape(shape),
        residual.astype(jnp.bfloat16).reshape(shape),
    )


def solution(mesh):
    placed = (
        P("sub", "reg", None, None),
        P("sub", "reg", None, None, None),
        P("sub", "reg", None, None),
        P("sub", "reg", None),
        P("sub", "reg", None),
        P("sub", "reg", None, None),
        P("sub", "reg", None, None),
        P("sub", "reg", None),
        P("reg", "sub", None),
    )
    return jax.shard_map(
        body,
        mesh=mesh,
        in_specs=placed,
        out_specs=(P("sub", "reg", None, None), P("sub", "reg", None, None)),
        check_vma=False,
    )
```

profile of v0, /device:TPU:0, one launch (start us, length us, event | category | flops | bytes accessed | tf_op | source)
XLA Modules:
  0.0 149.0 jit_solution(13466135424913627133)
XLA Ops:
  0.7 10.7 %all-gather = s32[1,1,1024]{2,1,0:T(1,128)S(1)} all-gather(s32[1,1,128]{2,1,0:T(1,128)} %param.22), channel_id=2, replica_groups=mesh['sub'=8,'reg'=4] {'sub'}, dimensions={2}, use_global_device_ids=true | all-gather | bytes 4608 | tf_op jit(solution)/shard_map/all_gather | solution.py:44
  12.4 4.0 %gather_fusion = f32[1024,64]{1,0:T(8,128)} fusion(f32[64,512]{0,1:T(8,128)S(1)} %bitcast.251, s32[1024]{0:T(1024)S(1)} %fusion.82), kind=kCustom, calls=%fused_computation.9 | custom fusion | bytes 528384 | tf_op jit(solution)/shard_map/jit(_take)/gather | solution.py:45
  18.3 3.4 %all-to-all-start = ((f32[64,8,128]{2,0,1:T(8,128)}), f32[64,8,128]{2,0,1:T(8,128)S(1)}, u32[]{:S(2)}, u32[]{:S(2)}) async-start(f32[64,8,128]{2,0,1:T(8,128)} %broadcast_select_fusion), calls=%async_computation | async-start | bytes 524288 | tf_op jit(solution)/shard_map/all_to_all | solution.py:48
  23.7 9.5 %all_gather.13 = f32[1024,16]{0,1:T(8,128)S(1)} all-gather(f32[128,16]{0,1:T(8,128)S(1)} %fusion.37), channel_id=1, replica_groups=mesh['sub'=8,'reg'=4] {'sub'}, dimensions={0}, use_global_device_ids=true | all-gather | bytes 73728 | tf_op jit(solution)/shard_map/all_gather | solution.py:58
  33.3 4.0 %gather_fusion.1 = f32[1024,128]{1,0:T(8,128)} fusion(f32[512,128]{1,0:T(8,128)S(1)} %bitcast.250, s32[1024]{0:T(1024)S(1)} %fusion.82), kind=kCustom, calls=%fused_computation.10 | custom fusion | bytes 1052672 | tf_op jit(solution)/shard_map/jit(_take)/gather | solution.py:50
  39.7 1.6 %collective-permute-start = (f32[128,16]{0,1:T(8,128)S(1)}, f32[128,16]{0,1:T(8,128)}, u32[]{:S(2)}, u32[]{:S(2)}) collective-permute-start(f32[128,16]{0,1:T(8,128)S(1)} %get-tuple-element.26), channel_id=1, source_target_pairs={{0,1},{1,2},{2,3},{3,0},{4,5},{5,6},{6,7},{7,4},{8,9},{9,10},{10,1... | collective-permute-start | bytes 24584 | tf_op jit(solution)/shard_map/ppermute | solution.py:11
  41.3 2.2 %collective-permute-start.1 = (f32[128,16]{0,1:T(8,128)S(1)}, f32[128,16]{0,1:T(8,128)}, u32[]{:S(2)}, u32[]{:S(2)}) collective-permute-start(f32[128,16]{0,1:T(8,128)S(1)} %get-tuple-element.25), channel_id=1, source_target_pairs={{0,3},{1,0},{2,1},{3,2},{4,7},{5,4},{6,5},{7,6},{8,11},{9,8},{10,9... | collective-permute-start | bytes 24584 | tf_op jit(solution)/shard_map/ppermute | solution.py:11
  43.6 3.8 %collective-permute-start.3 = (f32[128,16]{0,1:T(8,128)S(1)}, f32[128,16]{0,1:T(8,128)}, u32[]{:S(2)}, u32[]{:S(2)}) collective-permute-start(f32[128,16]{0,1:T(8,128)S(1)} %get-tuple-element.23), channel_id=1, source_target_pairs={{0,3},{1,0},{2,1},{3,2},{4,7},{5,4},{6,5},{7,6},{8,11},{9,8},{10,9... | collective-permute-start | bytes 24584 | tf_op jit(solution)/shard_map/ppermute | solution.py:11
  48.2 2.2 %fusion.11 = f32[80,128,16]{1,2,0:T(8,128)S(1)} fusion(bf16[1,1,80,128,128]{4,3,2,1,0:T(8,128)(2,1)S(1)} %copy-done, bf16[80,128,16]{1,2,0:T(8,128)(2,1)S(1)} %gather_fusion.2, pred[80]{0:T(512)(128)(4,1)} %get-tuple-element.4), kind=kOutput, calls=%fused_computation.25 | convolution fusion | flops 42106880 | bytes 3604560 | tf_op jit(solution)/shard_map/tij,tjr->tir/dot_general | solution.py:67
  51.5 2.6 %collective-permute-start.5 = (f32[128,16]{0,1:T(8,128)S(1)}, f32[128,16]{0,1:T(8,128)S(1)}, u32[]{:S(2)}, u32[]{:S(2)}) collective-permute-start(f32[128,16]{0,1:T(8,128)S(1)} %get-tuple-element.21), channel_id=1, source_target_pairs={{0,28},{4,0},{8,4},{12,8},{16,12},{20,16},{24,20},{28,24},{1,29},{... | collective-permute-start | bytes 24584 | tf_op jit(solution)/shard_map/ppermute | solution.py:11
  62.2 7.0 %gather_fusion.4 = f32[768,16]{1,0:T(8,128)} fusion(f32[6,128,16]{2,1,0:T(8,128)S(1)} %copy.35, s32[768]{0:T(1024)S(1)} %bitcast.246), kind=kCustom, calls=%fused_computation.2.clone | custom fusion | bytes 104448 | tf_op jit(solution)/shard_map/jit(take_along_axis)/gather | solution.py:79
  71.8 9.0 %all_gather.14 = f32[1024,16]{0,1:T(8,128)S(1)} all-gather(f32[128,16]{0,1:T(8,128)S(1)} %convolution_bitcast_fusion.4), channel_id=1, replica_groups=mesh['sub'=8,'reg'=4] {'sub'}, dimensions={0}, use_global_device_ids=true | all-gather | bytes 73728 | tf_op jit(solution)/shard_map/all_gather | solution.py:58
  84.2 2.4 %fusion.14 = f32[80,128,16]{1,2,0:T(8,128)} fusion(bf16[1,1,80,128,128]{4,3,2,1,0:T(8,128)(2,1)S(1)} %copy-done, bf16[80,128,16]{1,2,0:T(8,128)(2,1)S(1)} %gather_fusion.5, pred[80]{0:T(512)(128)(4,1)S(1)} %copy-done.13), kind=kOutput, calls=%fused_computation.26 | convolution fusion | flops 42106880 | bytes 3604560 | tf_op jit(solution)/shard_map/tij,tjr->tir/dot_general | solution.py:67
  87.3 2.2 %fusion.25 = f32[10,128,16]{1,0,2:T(8,128)} fusion(f32[80,128,16]{1,2,0:T(8,128)} %fusion.14, s32[80]{0:T(128)S(1)} %copy-done.12), kind=kOutput, calls=%fused_computation.41 | convolution fusion | flops 19661600 | bytes 737600 | tf_op jit(solution)/shard_map/bt,tir->bir/dot_general | solution.py:70
  89.5 3.8 %collective-permute-start.7 = (f32[128,16]{0,1:T(8,128)S(1)}, f32[128,16]{0,1:T(8,128)S(1)}, u32[]{:S(2)}, u32[]{:S(2)}) collective-permute-start(f32[128,16]{0,1:T(8,128)S(1)} %get-tuple-element.19), channel_id=1, source_target_pairs={{0,3},{1,0},{2,1},{3,2},{4,7},{5,4},{6,5},{7,6},{8,11},{9,8},{10,9... | collective-permute-start | bytes 24584 | tf_op jit(solution)/shard_map/ppermute | solution.py:11
  93.3 3.8 %collective-permute-start.9 = (f32[128,16]{0,1:T(8,128)S(1)}, f32[128,16]{0,1:T(8,128)S(1)}, u32[]{:S(2)}, u32[]{:S(2)}) collective-permute-start(f32[128,16]{0,1:T(8,128)S(1)} %get-tuple-element.17), channel_id=1, source_target_pairs={{0,3},{1,0},{2,1},{3,2},{4,7},{5,4},{6,5},{7,6},{8,11},{9,8},{10,9... | collective-permute-start | bytes 24584 | tf_op jit(solution)/shard_map/ppermute | solution.py:11
  97.1 2.6 %collective-permute-start.11 = (f32[128,16]{0,1:T(8,128)S(1)}, f32[128,16]{0,1:T(8,128)S(1)}, u32[]{:S(2)}, u32[]{:S(2)}) collective-permute-start(f32[128,16]{0,1:T(8,128)S(1)} %get-tuple-element.15), channel_id=1, source_target_pairs={{0,28},{4,0},{8,4},{12,8},{16,12},{20,16},{24,20},{28,24},{1,29},{... | collective-permute-start | bytes 24584 | tf_op jit(solution)/shard_map/ppermute | solution.py:11
  101.3 7.0 %gather_fusion.7 = f32[768,16]{1,0:T(8,128)} fusion(f32[6,128,16]{2,1,0:T(8,128)S(1)} %copy.40, s32[768]{0:T(1024)S(1)} %bitcast.247), kind=kCustom, calls=%fused_computation.7.clone | custom fusion | bytes 104448 | tf_op jit(solution)/shard_map/jit(take_along_axis)/gather | solution.py:79
  110.9 9.3 %all_gather.15 = f32[1024,16]{0,1:T(8,128)S(1)} all-gather(f32[128,16]{0,1:T(8,128)S(1)} %convolution_bitcast_fusion.3), channel_id=1, replica_groups=mesh['sub'=8,'reg'=4] {'sub'}, dimensions={0}, use_global_device_ids=true | all-gather | bytes 73728 | tf_op jit(solution)/shard_map/all_gather | solution.py:58
  123.4 2.4 %fusion.17 = f32[80,128,16]{1,2,0:T(8,128)} fusion(bf16[1,1,80,128,128]{4,3,2,1,0:T(8,128)(2,1)S(1)} %copy-done, bf16[80,128,16]{1,2,0:T(8,128)(2,1)S(1)} %gather_fusion.8, pred[80]{0:T(512)(128)(4,1)S(1)} %copy-done.13), kind=kOutput, calls=%fused_computation.27 | convolution fusion | flops 42106880 | bytes 3604560 | tf_op jit(solution)/shard_map/tij,tjr->tir/dot_general | solution.py:67
  128.0 3.9 %collective-permute-start.13 = (f32[128,16]{0,1:T(8,128)S(1)}, f32[128,16]{0,1:T(8,128)S(1)}, u32[]{:S(2)}, u32[]{:S(2)}) collective-permute-start(f32[128,16]{0,1:T(8,128)S(1)} %get-tuple-element.13), channel_id=1, source_target_pairs={{0,3},{1,0},{2,1},{3,2},{4,7},{5,4},{6,5},{7,6},{8,11},{9,8},{10,9... | collective-permute-start | bytes 24584 | tf_op jit(solution)/shard_map/ppermute | solution.py:11
  131.9 3.8 %collective-permute-start.15 = (f32[128,16]{0,1:T(8,128)S(1)}, f32[128,16]{0,1:T(8,128)S(1)}, u32[]{:S(2)}, u32[]{:S(2)}) collective-permute-start(f32[128,16]{0,1:T(8,128)S(1)} %get-tuple-element.11), channel_id=1, source_target_pairs={{0,3},{1,0},{2,1},{3,2},{4,7},{5,4},{6,5},{7,6},{8,11},{9,8},{10,9... | collective-permute-start | bytes 24584 | tf_op jit(solution)/shard_map/ppermute | solution.py:11
  135.7 2.6 %collective-permute-start.17 = (f32[128,16]{0,1:T(8,128)S(1)}, f32[128,16]{0,1:T(8,128)S(1)}, u32[]{:S(2)}, u32[]{:S(2)}) collective-permute-start(f32[128,16]{0,1:T(8,128)S(1)} %get-tuple-element.9), channel_id=1, source_target_pairs={{0,28},{4,0},{8,4},{12,8},{16,12},{20,16},{24,20},{28,24},{1,29},{... | collective-permute-start | bytes 24584 | tf_op jit(solution)/shard_map/ppermute | solution.py:11
  139.9 7.0 %gather_fusion.10 = f32[768,16]{1,0:T(8,128)} fusion(f32[6,128,16]{2,1,0:T(8,128)S(1)} %copy.45, s32[768]{0:T(1024)S(1)} %bitcast.248), kind=kCustom, calls=%fused_computation.8.clone | custom fusion | bytes 104448 | tf_op jit(solution)/shard_map/jit(take_along_axis)/gather | solution.py:79
  (133 shorter events, 37.1 us)
Async XLA Ops:
  0.6 47.5 %copy-start = (bf16[1,1,80,128,128]{4,3,2,1,0:T(8,128)(2,1)S(1)}, bf16[1,1,80,128,128]{4,3,2,1,0:T(8,128)(2,1)}, u32[]{:S(2)}) copy-start(bf16[1,1,80,128,128]{4,3,2,1,0:T(8,128)(2,1)} %param.16) | copy-start | bytes 7864324
  0.7 22.2 %copy-start.5 = (s32[1,1,6,128]{3,1,2,0:T(1,128)S(1)}, s32[1,1,6,128]{3,1,2,0:T(1,128)}, u32[]{:S(2)}) copy-start(s32[1,1,6,128]{3,1,2,0:T(1,128)} %param.20) | copy-start | bytes 9220
  0.7 22.2 %copy-start.1 = (bf16[1,1,1280,128]{3,2,1,0:T(8,128)(2,1)S(1)}, bf16[1,1,1280,128]{3,2,1,0:T(8,128)(2,1)}, u32[]{:S(2)}) copy-start(bf16[1,1,1280,128]{3,2,1,0:T(8,128)(2,1)} %param.21) | copy-start | bytes 983044
  0.7 22.2 %copy-start.2 = (f32[1,1,1280,16]{2,3,1,0:T(8,128)S(1)}, f32[1,1,1280,16]{2,3,1,0:T(8,128)}, u32[]{:S(2)}) copy-start(f32[1,1,1280,16]{2,3,1,0:T(8,128)} %param.15) | copy-start | bytes 245764
  0.7 32.5 %copy-start.6 = (f32[1,1,1280]{2,1,0:T(1,128)S(1)}, f32[1,1,1280]{2,1,0:T(1,128)}, u32[]{:S(2)}) copy-start(f32[1,1,1280]{2,1,0:T(1,128)} %param.18) | copy-start | bytes 15364
  18.3 14.9 %all-to-all-start = ((f32[64,8,128]{2,0,1:T(8,128)}), f32[64,8,128]{2,0,1:T(8,128)S(1)}, u32[]{:S(2)}, u32[]{:S(2)}) async-start(f32[64,8,128]{2,0,1:T(8,128)} %broadcast_select_fusion), calls=%async_computation | async-start | bytes 524288 | tf_op jit(solution)/shard_map/all_to_all | solution.py:48
  39.7 11.8 %collective-permute-start = (f32[128,16]{0,1:T(8,128)S(1)}, f32[128,16]{0,1:T(8,128)}, u32[]{:S(2)}, u32[]{:S(2)}) collective-permute-start(f32[128,16]{0,1:T(8,128)S(1)} %get-tuple-element.26), channel_id=1, source_target_pairs={{0,1},{1,2},{2,3},{3,0},{4,5},{5,6},{6,7},{7,4},{8,9},{9,10},{10,1... | collective-permute-start | bytes 24584 | tf_op jit(solution)/shard_map/ppermute | solution.py:11
  41.3 14.2 %collective-permute-start.1 = (f32[128,16]{0,1:T(8,128)S(1)}, f32[128,16]{0,1:T(8,128)}, u32[]{:S(2)}, u32[]{:S(2)}) collective-permute-start(f32[128,16]{0,1:T(8,128)S(1)} %get-tuple-element.25), channel_id=1, source_target_pairs={{0,3},{1,0},{2,1},{3,2},{4,7},{5,4},{6,5},{7,6},{8,11},{9,8},{10,9... | collective-permute-start | bytes 24584 | tf_op jit(solution)/shard_map/ppermute | solution.py:11
  43.6 13.2 %collective-permute-start.2 = (f32[128,16]{0,1:T(8,128)S(1)}, f32[128,16]{0,1:T(8,128)}, u32[]{:S(2)}, u32[]{:S(2)}) collective-permute-start(f32[128,16]{0,1:T(8,128)S(1)} %get-tuple-element.24), channel_id=1, source_target_pairs={{0,1},{1,2},{2,3},{3,0},{4,5},{5,6},{6,7},{7,4},{8,9},{9,10},{10,1... | collective-permute-start | bytes 24584 | tf_op jit(solution)/shard_map/ppermute | solution.py:11
  43.6 14.5 %collective-permute-start.3 = (f32[128,16]{0,1:T(8,128)S(1)}, f32[128,16]{0,1:T(8,128)}, u32[]{:S(2)}, u32[]{:S(2)}) collective-permute-start(f32[128,16]{0,1:T(8,128)S(1)} %get-tuple-element.23), channel_id=1, source_target_pairs={{0,3},{1,0},{2,1},{3,2},{4,7},{5,4},{6,5},{7,6},{8,11},{9,8},{10,9... | collective-permute-start | bytes 24584 | tf_op jit(solution)/shard_map/ppermute | solution.py:11
  47.4 12.0 %collective-permute-start.4 = (f32[128,16]{0,1:T(8,128)S(1)}, f32[128,16]{0,1:T(8,128)}, u32[]{:S(2)}, u32[]{:S(2)}) collective-permute-start(f32[128,16]{0,1:T(8,128)S(1)} %get-tuple-element.22), channel_id=1, source_target_pairs={{0,4},{4,8},{8,12},{12,16},{16,20},{20,24},{24,28},{28,0},{1,5},{5... | collective-permute-start | bytes 24584 | tf_op jit(solution)/shard_map/ppermute | solution.py:11
  51.5 9.1 %collective-permute-start.5 = (f32[128,16]{0,1:T(8,128)S(1)}, f32[128,16]{0,1:T(8,128)S(1)}, u32[]{:S(2)}, u32[]{:S(2)}) collective-permute-start(f32[128,16]{0,1:T(8,128)S(1)} %get-tuple-element.21), channel_id=1, source_target_pairs={{0,28},{4,0},{8,4},{12,8},{16,12},{20,16},{24,20},{28,24},{1,29},{... | collective-permute-start | bytes 24584 | tf_op jit(solution)/shard_map/ppermute | solution.py:11
  87.2 9.9 %collective-permute-start.6 = (f32[128,16]{0,1:T(8,128)S(1)}, f32[128,16]{0,1:T(8,128)S(1)}, u32[]{:S(2)}, u32[]{:S(2)}) collective-permute-start(f32[128,16]{0,1:T(8,128)S(1)} %get-tuple-element.20), channel_id=1, source_target_pairs={{0,1},{1,2},{2,3},{3,0},{4,5},{5,6},{6,7},{7,4},{8,9},{9,10},{10,1... | collective-permute-start | bytes 24584 | tf_op jit(solution)/shard_map/ppermute | solution.py:11
  89.5 10.3 %collective-permute-start.7 = (f32[128,16]{0,1:T(8,128)S(1)}, f32[128,16]{0,1:T(8,128)S(1)}, u32[]{:S(2)}, u32[]{:S(2)}) collective-permute-start(f32[128,16]{0,1:T(8,128)S(1)} %get-tuple-element.19), channel_id=1, source_target_pairs={{0,3},{1,0},{2,1},{3,2},{4,7},{5,4},{6,5},{7,6},{8,11},{9,8},{10,9... | collective-permute-start | bytes 24584 | tf_op jit(solution)/shard_map/ppermute | solution.py:11
  93.3 6.5 %collective-permute-start.8 = (f32[128,16]{0,1:T(8,128)S(1)}, f32[128,16]{0,1:T(8,128)S(1)}, u32[]{:S(2)}, u32[]{:S(2)}) collective-permute-start(f32[128,16]{0,1:T(8,128)S(1)} %get-tuple-element.18), channel_id=1, source_target_pairs={{0,1},{1,2},{2,3},{3,0},{4,5},{5,6},{6,7},{7,4},{8,9},{9,10},{10,1... | collective-permute-start | bytes 24584 | tf_op jit(solution)/shard_map/ppermute | solution.py:11
  93.3 6.5 %collective-permute-start.9 = (f32[128,16]{0,1:T(8,128)S(1)}, f32[128,16]{0,1:T(8,128)S(1)}, u32[]{:S(2)}, u32[]{:S(2)}) collective-permute-start(f32[128,16]{0,1:T(8,128)S(1)} %get-tuple-element.17), channel_id=1, source_target_pairs={{0,3},{1,0},{2,1},{3,2},{4,7},{5,4},{6,5},{7,6},{8,11},{9,8},{10,9... | collective-permute-start | bytes 24584 | tf_op jit(solution)/shard_map/ppermute | solution.py:11
  97.1 4.0 %collective-permute-start.10 = (f32[128,16]{0,1:T(8,128)S(1)}, f32[128,16]{0,1:T(8,128)S(1)}, u32[]{:S(2)}, u32[]{:S(2)}) collective-permute-start(f32[128,16]{0,1:T(8,128)S(1)} %get-tuple-element.16), channel_id=1, source_target_pairs={{0,4},{4,8},{8,12},{12,16},{16,20},{20,24},{24,28},{28,0},{1,5},{5... | collective-permute-start | bytes 24584 | tf_op jit(solution)/shard_map/ppermute | solution.py:11
  97.1 4.0 %collective-permute-start.11 = (f32[128,16]{0,1:T(8,128)S(1)}, f32[128,16]{0,1:T(8,128)S(1)}, u32[]{:S(2)}, u32[]{:S(2)}) collective-permute-start(f32[128,16]{0,1:T(8,128)S(1)} %get-tuple-element.15), channel_id=1, source_target_pairs={{0,28},{4,0},{8,4},{12,8},{16,12},{20,16},{24,20},{28,24},{1,29},{... | collective-permute-start | bytes 24584 | tf_op jit(solution)/shard_map/ppermute | solution.py:11
  126.4 9.3 %collective-permute-start.12 = (f32[128,16]{0,1:T(8,128)S(1)}, f32[128,16]{0,1:T(8,128)S(1)}, u32[]{:S(2)}, u32[]{:S(2)}) collective-permute-start(f32[128,16]{0,1:T(8,128)S(1)} %get-tuple-element.14), channel_id=1, source_target_pairs={{0,1},{1,2},{2,3},{3,0},{4,5},{5,6},{6,7},{7,4},{8,9},{9,10},{10,1... | collective-permute-start | bytes 24584 | tf_op jit(solution)/shard_map/ppermute | solution.py:11
  128.0 10.3 %collective-permute-start.13 = (f32[128,16]{0,1:T(8,128)S(1)}, f32[128,16]{0,1:T(8,128)S(1)}, u32[]{:S(2)}, u32[]{:S(2)}) collective-permute-start(f32[128,16]{0,1:T(8,128)S(1)} %get-tuple-element.13), channel_id=1, source_target_pairs={{0,3},{1,0},{2,1},{3,2},{4,7},{5,4},{6,5},{7,6},{8,11},{9,8},{10,9... | collective-permute-start | bytes 24584 | tf_op jit(solution)/shard_map/ppermute | solution.py:11
  131.9 6.5 %collective-permute-start.14 = (f32[128,16]{0,1:T(8,128)S(1)}, f32[128,16]{0,1:T(8,128)S(1)}, u32[]{:S(2)}, u32[]{:S(2)}) collective-permute-start(f32[128,16]{0,1:T(8,128)S(1)} %get-tuple-element.12), channel_id=1, source_target_pairs={{0,1},{1,2},{2,3},{3,0},{4,5},{5,6},{6,7},{7,4},{8,9},{9,10},{10,1... | collective-permute-start | bytes 24584 | tf_op jit(solution)/shard_map/ppermute | solution.py:11
  131.9 6.5 %collective-permute-start.15 = (f32[128,16]{0,1:T(8,128)S(1)}, f32[128,16]{0,1:T(8,128)S(1)}, u32[]{:S(2)}, u32[]{:S(2)}) collective-permute-start(f32[128,16]{0,1:T(8,128)S(1)} %get-tuple-element.11), channel_id=1, source_target_pairs={{0,3},{1,0},{2,1},{3,2},{4,7},{5,4},{6,5},{7,6},{8,11},{9,8},{10,9... | collective-permute-start | bytes 24584 | tf_op jit(solution)/shard_map/ppermute | solution.py:11
  135.7 4.0 %collective-permute-start.16 = (f32[128,16]{0,1:T(8,128)S(1)}, f32[128,16]{0,1:T(8,128)S(1)}, u32[]{:S(2)}, u32[]{:S(2)}) collective-permute-start(f32[128,16]{0,1:T(8,128)S(1)} %get-tuple-element.10), channel_id=1, source_target_pairs={{0,4},{4,8},{8,12},{12,16},{16,20},{20,24},{24,28},{28,0},{1,5},{5... | collective-permute-start | bytes 24584 | tf_op jit(solution)/shard_map/ppermute | solution.py:11
  135.7 4.0 %collective-permute-start.17 = (f32[128,16]{0,1:T(8,128)S(1)}, f32[128,16]{0,1:T(8,128)S(1)}, u32[]{:S(2)}, u32[]{:S(2)}) collective-permute-start(f32[128,16]{0,1:T(8,128)S(1)} %get-tuple-element.9), channel_id=1, source_target_pairs={{0,28},{4,0},{8,4},{12,8},{16,12},{20,16},{24,20},{28,24},{1,29},{... | collective-permute-start | bytes 24584 | tf_op jit(solution)/shard_map/ppermute | solution.py:11
  (10 other events, 109.0 us)
where the time goes:
time: 150 us; the launch traced here: 149 us
  local copies, waits for them, and re-layouts  48.4 us (32%)
  blocking collectives  38.5 us (26%)
  starting transfers between devices  34.5 us (23%)
  matrix products  20.4 us (14%)
  other arithmetic  3.46 us (2%)
  waiting for transfers between devices  2.68 us (2%)
    ppermute x18, starting transfers between devices, from_behind(): lax.ppermute(shard, axis, [(i, (i + by) % peers) for i in range(peers)])  31.1 us
    all_gather x3, blocking collectives, body(): lax.all_gather(local_coarse, 'sub', axis=0, tiled=True)  27.8 us
    gather x6, local copies, waits for them, and re-layouts, body(): permuted = jnp.take_along_axis(received, matched[:, :, None], axis=1)  24.4 us
    all_gather x1, blocking collectives, body(): every_ids = lax.all_gather(own_map, 'sub', axis=0, tiled=True)  10.7 us
    unnamed x47, local copies, waits for them, and re-layouts  8.21 us
    dot_general x3, matrix products, body(): jnp.einsum('tij,tjr->tir', tile_block, picked, preferred_element_type=jnp...  6.87 us
    gather x2, local copies, waits for them, and re-layouts, body(): jnp.take(inverse_rows, every_ids, axis=1)  5.21 us
    dot_general x3, matrix products, body(): jnp.einsum('bt,tir->bir', row_table, products, precision=lax.Precision.HI...  4.98 us
  transfers between devices with their start and end apart: 19, of which 2 were waited for; matrix products, arithmetic and copies ran while one was open for 11% of the time, Pallas kernels for 0%

commit v1 on v0

v1 whole, which is shorter than its diff:
```python
import functools

import jax
import jax.numpy as jnp
from jax import lax
from jax.experimental import pallas as pl
from jax.experimental.pallas import tpu as pltpu
from jax.sharding import PartitionSpec as P

SWEEPS = 3
F32 = jnp.float32
BF16 = jnp.bfloat16
I32 = jnp.int32
VMEM = pl.BlockSpec(memory_space=pltpu.VMEM)
ANY = pl.BlockSpec(memory_space=pl.ANY)
SMEM = pl.BlockSpec(memory_space=pltpu.SMEM)
NT = (((1,), (1,)), ((), ()))
NN = (((1,), (0,)), ((), ()))


def matmul(a, b, dims):
    return lax.dot_general(a, b, dims, preferred_element_type=F32)


def at_block(block, tile):
    return pl.ds(pl.multiple_of(block * tile, tile), tile)


def lanes(ref):
    return jnp.concatenate([ref[b] for b in range(ref.shape[0])], axis=1)


def one_hot(mask):
    return mask.astype(F32).astype(BF16)


def put_all(ref, value):
    def put(i, carry):
        ref[i] = value
        return carry

    lax.fori_loop(0, ref.shape[0], put, 0, unroll=min(8, ref.shape[0]))


def first_kernel(place_ref, rhs_ref, basis_ref, inverse_ref, ids_ref, chunk_ref):
    rights = rhs_ref.shape[0]
    held, total = inverse_ref.shape
    coarse = matmul(rhs_ref[...].astype(BF16), basis_ref[...], NN)
    ids = ids_ref[...]
    high = (ids // 128).astype(F32)
    low = (ids % 128).astype(F32)
    count = ids.shape[1]
    own_diagonal = lax.broadcasted_iota(I32, (held, total), 1) == (
        lax.broadcasted_iota(I32, (held, total), 0) + place_ref[0] * held
    )
    rows = inverse_ref[...]
    rounded = rows.astype(BF16)
    dropped = jnp.where(own_diagonal, rows - rounded.astype(F32), 0.0)
    dropped = jnp.sum(dropped, axis=0, keepdims=True)
    codes = [high, low] + [dropped[:, q * count : (q + 1) * count] for q in range(total // count)]
    code_rows = -(-len(codes) // 16) * 16
    row = lax.broadcasted_iota(I32, (code_rows, count), 0)
    coded = jnp.zeros((code_rows, count), F32)
    for n, code in enumerate(codes):
        coded = jnp.where(row == n, code, coded)
    pieces = [coded.astype(BF16), coarse.astype(BF16)]
    for q in range(total // count):
        pieces.append(rounded[:, q * count : (q + 1) * count])
    put_all(chunk_ref, jnp.concatenate(pieces, axis=0))


def update(z, basis_ref, weights_ref, u, r, place_ref, faces_ref, new_ref, low_ref, out_refs, groups):
    tile = out_refs[0].shape[2]
    value = weights_ref[...] * r + matmul(z.astype(BF16), basis_ref[...], NT)
    if u is not None:
        value = u + value
    new_ref[...] = value
    low_ref[...] = value.astype(BF16)
    for out_ref, (faces, turn) in zip(out_refs, groups, strict=True):
        for n, face in enumerate(faces):
            out_ref[n] = low_ref[:, at_block(faces_ref[0, face ^ place_ref[turn]], tile)]


def opening_kernel(
    groups,
    total,
    place_ref,
    faces_ref,
    tiles_ref,
    ids_ref,
    got_ref,
    basis_ref,
    weights_ref,
    r_ref,
    kept_ref,
    block_ref,
    new_ref,
    low_ref,
    *refs,
):
    *out_refs, sem = refs
    copy = pltpu.make_async_copy(tiles_ref, kept_ref, sem)
    copy.start()
    peers = got_ref.shape[0]
    rights = r_ref.shape[0]
    count = ids_ref.shape[1]
    parts = total // count
    code_rows = -(-(2 + parts) // 16) * 16
    body_at = code_rows + rights
    held = (got_ref.shape[1] - body_at) // parts
    codes = [got_ref[i, :code_rows, :].astype(F32) for i in range(peers)]
    dropped = sum(codes)
    column = jnp.broadcast_to(ids_ref[...].astype(F32), (count, count)).T
    lane = lax.broadcasted_iota(I32, (count, count), 1).astype(F32)
    own = [column == lane + float(q * count) for q in range(parts)]
    own_low = jnp.concatenate([one_hot(hot) for hot in own], axis=1)
    own_rows, own_dropped = [], []
    for q in range(parts):
        piece = got_ref[:, body_at + q * held : body_at + (q + 1) * held, :].reshape(peers * held, count)
        own_rows.append(matmul(own_low, piece, NN).astype(BF16))
        own_dropped.append(jnp.where(own[q], dropped[2 + q : 3 + q], 0.0).astype(BF16))
    own_rows = jnp.concatenate(
        [jnp.concatenate(own_rows, axis=1), jnp.concatenate(own_dropped, axis=1)], axis=0
    )
    index = lax.broadcasted_iota(I32, (total, count), 0).astype(F32)
    z = jnp.zeros((rights, count), F32)
    for i in range(peers):
        ids = codes[i][0:1] * 128.0 + codes[i][1:2]
        piece = matmul(own_rows, one_hot(index == ids), NN).astype(BF16)
        block_ref[i] = piece
        both = matmul(got_ref[i, code_rows:body_at, :], piece, NT)
        z = z + both[:, :count] + both[:, count:]
    update(z, basis_ref, weights_ref, None, r_ref[...], place_ref, faces_ref, new_ref, low_ref, out_refs, groups)
    copy.wait()


def correct_kernel(
    groups, place_ref, faces_ref, got_ref, block_ref, basis_ref, weights_ref, u_ref, r_ref, new_ref, low_ref, *out_refs
):
    count = got_ref.shape[2]
    both = matmul(lanes(got_ref), lanes(block_ref), NT)
    z = both[:, :count] + both[:, count:]
    update(z, basis_ref, weights_ref, u_ref[...], r_ref[...], place_ref, faces_ref, new_ref, low_ref, out_refs, groups)


def local_kernel(list_ref, x_ref, tiles_ref, y_ref):
    tile = tiles_ref.shape[1]
    for t in range(tiles_ref.shape[0]):
        product = matmul(x_ref[:, at_block(list_ref[1, t], tile)], tiles_ref[t], NT)
        cut = at_block(list_ref[0, t], tile)
        if t * tile < y_ref.shape[1]:
            y_ref[:, t * tile : (t + 1) * tile] = product
        else:
            y_ref[:, cut] = y_ref[:, cut] + product


def couple(groups, place_ref, faces_ref, match_ref, rhs_ref, y_ref, in_refs, r_ref):
    tile = match_ref.shape[2]
    r_ref[...] = rhs_ref[...] - y_ref[...]
    index = lax.broadcasted_iota(I32, (tile, tile), 0)
    for in_ref, (faces, turn) in zip(in_refs, groups, strict=True):
        for n, first in enumerate(faces):
            face = first ^ place_ref[turn]
            got = matmul(in_ref[n], one_hot(index == match_ref[face]), NN)
            cut = at_block(faces_ref[0, face], tile)
            r_ref[:, cut] = r_ref[:, cut] + 0.5 * got


def residual_kernel(groups, place_ref, faces_ref, match_ref, rhs_ref, y_ref, basis_ref, *refs):
    in_refs, (r_ref, chunk_ref) = refs[: len(groups)], refs[len(groups) :]
    couple(groups, place_ref, faces_ref, match_ref, rhs_ref, y_ref, in_refs, r_ref)
    put_all(chunk_ref, matmul(r_ref[...].astype(BF16), basis_ref[...], NN).astype(BF16))


def last_kernel(groups, place_ref, faces_ref, match_ref, rhs_ref, y_ref, *refs):
    in_refs, (out_ref, r_ref) = refs[: len(groups)], refs[len(groups) :]
    couple(groups, place_ref, faces_ref, match_ref, rhs_ref, y_ref, in_refs, r_ref)
    out_ref[...] = r_ref[...].astype(BF16)


def near(*arrays):
    return [pltpu.with_memory_space_constraint(a, pltpu.VMEM) for a in arrays]


def call(kernel, outs, scalars, *args, scratch=(), far=()):
    return pl.pallas_call(
        kernel,
        out_shape=outs,
        in_specs=[SMEM] * len(scalars) + [ANY] * len(far) + [VMEM] * len(args),
        out_specs=[VMEM] * len(outs),
        scratch_shapes=list(scratch),
        compiler_params=pltpu.CompilerParams(vmem_limit_bytes=16 << 20),
    )(*scalars, *far, *args)


def body(
    right_side,
    tiles,
    tile_list,
    weights,
    face_map,
    matching,
    coarse_basis,
    coarse_map,
    coarse_inverse,
):
    order, rights = right_side.shape[2:]
    tile = tiles.shape[3]
    listing = tile_list[0, 0].T
    scaling = weights[0]
    faces_here = face_map[0]
    ids = coarse_map[0]
    count = ids.shape[1]
    inverse_rows = coarse_inverse[0]
    held, total = inverse_rows.shape
    peers = lax.axis_size("sub")
    stride = max(lax.axis_size("reg") // 4, 1)
    place = jnp.stack(
        [lax.axis_index("sub"), lax.axis_index("sub") % 2]
        + [lax.axis_index("reg") // far % 2 for far in sorted({1, stride})]
    ).astype(I32)
    if stride == 1:
        swaps = (((0, 2), "reg", 1, False, 2), ((1, 3), "reg", 1, True, 2))
    else:
        swaps = (
            ((0,), "reg", 1, False, 2),
            ((2,), "reg", stride, False, 3),
            ((1,), "reg", 1, True, 2),
            ((3,), "reg", stride, True, 3),
        )
    swaps = ((((4,), "sub", 1, False, 1),) + swaps + (((5,), "sub", 1, True, 1),))
    groups = tuple((faces, turn) for faces, _, _, _, turn in swaps)

    def swap(shard, axis, far, ahead):
        n = lax.axis_size(axis)
        assert n // far % 2 == 0
        pairs = []
        for i in range(n):
            if (i // far % 2 == 0) == ahead:
                pairs += [(i, (i + far) % n), ((i + far) % n, i)]
        return lax.ppermute(shard, axis, pairs)

    near_out, far_out = pltpu.VMEM, jax.ShapeDtypeStruct
    field = near_out((rights, order), F32)
    field_low = near_out((rights, order), BF16)
    face_outs = [far_out((len(faces), rights, tile), BF16) for faces, _ in groups]
    parts = total // count
    rows = -(-(2 + parts) // 16) * 16 + rights + held * parts

    def spread(chunk):
        return near(lax.all_to_all(chunk, "sub", split_axis=0, concat_axis=0, tiled=True))[0]

    rhs, basis, matched = near(right_side[0, 0].T, coarse_basis[0, 0], matching[0].reshape(-1, 1, tile))
    (chunk,) = call(
        first_kernel, [far_out((peers, rows, count), BF16)], [place], rhs, basis, inverse_rows, ids
    )
    residual = rhs
    got = spread(chunk)
    for sweep in range(SWEEPS):
        if sweep == 0:
            tile_block, block, u, low, *faces = call(
                functools.partial(opening_kernel, groups, total),
                [
                    near_out(tiles.shape[2:], BF16),
                    near_out((peers, 2 * count, count), BF16),
                    field,
                    field_low,
                    *face_outs,
                ],
                [place, faces_here],
                ids,
                got,
                basis,
                scaling,
                residual,
                far=[tiles[0, 0]],
                scratch=[pltpu.SemaphoreType.DMA],
            )
        else:
            u, low, *faces = call(
                functools.partial(correct_kernel, groups),
                [field, field_low, *face_outs],
                [place, faces_here],
                got,
                block,
                basis,
                scaling,
                u,
                residual,
            )
        arrived = near(*[swap(f, *how[1:4]) for f, how in zip(faces, swaps, strict=True)])
        (local,) = call(local_kernel, [field], [listing], low, tile_block)
        if sweep + 1 < SWEEPS:
            residual, chunk = call(
                functools.partial(residual_kernel, groups),
                [field, far_out((peers, rights, count), BF16)],
                [place, faces_here],
                matched,
                rhs,
                local,
                basis,
                *arrived,
            )
            got = spread(chunk)
        else:
            (left,) = call(
                functools.partial(last_kernel, groups),
                [jax.ShapeDtypeStruct((rights, order), BF16)],
                [place, faces_here],
                matched,
                rhs,
                local,
                *arrived,
                scratch=[pltpu.VMEM((rights, order), F32)],
            )
    return low.T[None, None], left.T[None, None]


def solution(mesh):
    placed = (
        P("sub", "reg", None, None),
        P("sub", "reg", None, None, None),
        P("sub", "reg", None, None),
        P("sub", "reg", None),
        P("sub", "reg", None),
        P("sub", "reg", None, None),
        P("sub", "reg", None, None),
        P("sub", "reg", None),
        P("reg", "sub", None),
    )
    return jax.shard_map(
        body,
        mesh=mesh,
        in_specs=placed,
        out_specs=(P("sub", "reg", None, None), P("sub", "reg", None, None)),
        check_vma=False,
    )
```

time: 150 us -> 68.5 us (0.46)
  local copies, waits for them, and re-layouts: 48.4 us -> 7.81 us
  starting transfers between devices: 34.5 us -> 10.7 us
  matrix products: 20.4 us -> 0 us
  Pallas kernels: 0 us -> 15.7 us
  blocking collectives: 38.5 us -> 30 us
  other arithmetic: 3.46 us -> 0.08 us
    all_gather x4 -> x0, blocking collectives: 38.5 us -> none  [the longest x3 27.8 us: body(): lax.all_gather(local_coarse, 'sub', axis=0, tiled=True)]
    gather x15 -> x0, local copies, waits for them, and re-layouts: 37.7 us -> none  [the longest x6 24.4 us: body(): permuted = jnp.take_along_axis(received, matched[:, :, None], axis=1)]
    all_to_all x0 -> x3, blocking collectives: none -> 30 us  [spread(): lax.all_to_all(chunk, 'sub', split_axis=0, concat_axis=0, tiled=True)]
    dot_general x18 -> x0, matrix products: 20.4 us -> none  [the longest x3 6.87 us: body(): jnp.einsum('tij,tjr->tir', tile_block, picked, preferred_element_type=jnp...]
    ppermute x18 -> x12, starting transfers between devices: 31.1 us -> 10.7 us  [swap(): return lax.ppermute(shard, axis, pairs)]
    pallas_call x0 -> x10, Pallas kernels: none -> 15.7 us  [call(): pl.pallas_call(kernel, out_shape=outs, in_specs=[SMEM] * len(scalars) + [...]
    all_to_all x1 -> x0, starting transfers between devices: 3.41 us -> none  [body(): lax.all_to_all(outgoing_part, 'sub', split_axis=1, concat_axis=0, tiled=T...]
    another operation x6 -> x0, local copies, waits for them, and re-layouts: 1.88 us -> none  [body(): received = jnp.stack(arrived)]
  transfers between devices with their start and end apart: 19 -> 12, of which waited for: 2 -> 3; matrix products, arithmetic and copies ran while one was open for 11% -> 1% of each run, Pallas kernels for 0% -> 9%
where the time goes in v1:
time: 68.5 us; the launch traced here: 68.1 us
  blocking collectives  30 us (44%)
  Pallas kernels  15.7 us (23%)
  starting transfers between devices  10.7 us (16%)
  local copies, waits for them, and re-layouts  7.81 us (11%)
  waiting for transfers between devices  3.1 us (5%)
  between operations  0.73 us (1%)
    all_to_all x3, blocking collectives, spread(): lax.all_to_all(chunk, 'sub', split_axis=0, concat_axis=0, tiled=True)  30 us
    pallas_call x10, Pallas kernels, call(): pl.pallas_call(kernel, out_shape=outs, in_specs=[SMEM] * len(scalars) + [...  15.7 us
    ppermute x12, starting transfers between devices, swap(): return lax.ppermute(shard, axis, pairs)  10.7 us
    unnamed x25, local copies, waits for them, and re-layouts  7.81 us
    ppermute x12, waiting for transfers between devices, swap(): return lax.ppermute(shard, axis, pairs)  3.1 us
  transfers between devices with their start and end apart: 12, of which 3 were waited for; matrix products, arithmetic and copies ran while one was open for 1% of the time, Pallas kernels for 9%

profile of v1, /device:TPU:0, one launch (start us, length us, event | category | flops | bytes accessed | tf_op | source)
XLA Modules:
  0.0 68.1 jit_solution(14864035696947402001)
XLA Ops:
  0.7 1.0 %copy-done = bf16[1,1,1280,128]{3,2,1,0:T(8,128)(2,1)S(1)} copy-done((bf16[1,1,1280,128]{3,2,1,0:T(8,128)(2,1)S(1)}, bf16[1,1,1280,128]{3,2,1,0:T(8,128)(2,1)}, u32[]{:S(2)}) %copy-start) | copy-done | bytes 327704
  1.7 0.9 %copy-done.3 = f32[1,1,1280,16]{2,3,1,0:T(8,128)S(1)} copy-done((f32[1,1,1280,16]{2,3,1,0:T(8,128)S(1)}, f32[1,1,1280,16]{2,3,1,0:T(8,128)}, u32[]{:S(2)}) %copy-start.3) | copy-done | bytes 81944
  2.6 0.9 %copy-done.4 = f32[1,64,512]{2,1,0:T(8,128)S(1)} copy-done((f32[1,64,512]{2,1,0:T(8,128)S(1)}, f32[1,64,512]{2,1,0:T(8,128)}, u32[]{:S(2)}) %copy-start.4) | copy-done | bytes 131096
  4.1 0.7 %shard_map.104 = bf16[8,288,128]{2,1,0:T(8,128)(2,1)S(1)} custom-call(s32[3]{0:T(128)S(1)} %pad_add_fusion.place_ref, f32[16,1280]{1,0:T(8,128)S(1)} %bitcast.30, bf16[1280,128]{1,0:T(8,128)(2,1)S(1)} %bitcast.23, f32[64,512]{1,0:T(8,128)S(1)} %bitcast.35, s32[1,128]{1,0:T(1,128)S(1)} %bitcast.51), custom_call_target="tpu_custom_call" | custom-call | tf_op jit(solution)/shard_map/pallas_call | solution.py:186
  4.9 15.5 %all_to_all.15.got_ref = bf16[8,288,128]{2,1,0:T(8,128)(2,1)S(1)} all-to-all(bf16[8,288,128]{2,1,0:T(8,128)(2,1)S(1)} %shard_map.104), channel_id=1, replica_groups=mesh['sub'=8,'reg'=4] {'sub'}, dimensions={0} | all-to-all | bytes 1179648 | tf_op jit(solution)/shard_map/all_to_all | solution.py:251
  20.4 1.7 %copy-done.2 = bf16[1,1,80,128,128]{4,3,2,1,0:T(8,128)(2,1)S(1)} copy-done((bf16[1,1,80,128,128]{4,3,2,1,0:T(8,128)(2,1)S(1)}, bf16[1,1,80,128,128]{4,3,2,1,0:T(8,128)(2,1)}, u32[]{:S(2)}) %copy-start.2) | copy-done | bytes 2621464
  22.1 0.7 %copy-done.5 = f32[1,1,1280]{2,1,0:T(1,128)S(1)} copy-done((f32[1,1,1280]{2,1,0:T(1,128)S(1)}, f32[1,1,1280]{2,1,0:T(1,128)}, u32[]{:S(2)}) %copy-start.5) | copy-done | bytes 5144
  24.1 3.0 %shard_map.105 = (bf16[80,128,128]{2,1,0:T(8,128)(2,1)S(1)}, bf16[8,256,128]{2,1,0:T(8,128)(2,1)S(1)}, f32[16,1280]{1,0:T(8,128)S(1)}, bf16[16,1280]{1,0:T(8,128...) custom-call(s32[3]{0:T(128)S(1)} %pad_add_fusion.place_ref, ...), custom_call_target="tpu_custom_call" | custom-call | tf_op jit(solution)/shard_map/pallas_call | solution.py:186
  27.1 3.7 %collective-permute-start.1 = (bf16[2,16,128]{2,1,0:T(8,128)(2,1)S(1)}, bf16[2,16,128]{2,1,0:T(8,128)(2,1)S(1)}, u32[]{:S(2)}, u32[]{:S(2)}) collective-permute-start(bf16[2,16,128]{2,1,0:T(8,128)(2,1)S(1)} %get-tuple-element.28), channel_id=1, source_target_pairs={{1,2},{2,1},{3,0},{0,3},{5,6},{6,5},{7,4},{4,7},{9,10},{10,9},{11,... | collective-permute-start | bytes 24584 | tf_op jit(solution)/shard_map/ppermute | solution.py:241
  30.8 0.7 collective-permute-start.3
  31.5 2.0 %shard_map.106.y_ref = f32[16,1280]{1,0:T(8,128)S(1)} custom-call(s32[2,80]{1,0:T(2,128)S(1)} %bitcast.48, bf16[16,1280]{1,0:T(8,128)(2,1)S(1)} %get-tuple-element.25.x_ref, bf16[80,128,128]{2,1,0:T(8,128)(2,1)S(1)} %get-tuple-element.26.tiles_ref), custom_call_target="tpu_custom_call" | custom-call | tf_op jit(solution)/shard_map/pallas_call | solution.py:186
  33.5 1.2 %collective-permute-done.refs_0_ = bf16[1,16,128]{2,1,0:T(8,128)(2,1)S(1)} collective-permute-done((bf16[1,16,128]{2,1,0:T(8,128)(2,1)S(1)}, bf16[1,16,128]{2,1,0:T(8,128)(2,1)S(1)}, u32[]{:S(2)}, u32[]{:S(2)}) %collective-permute-start) | collective-permute-done | bytes 4128 | tf_op jit(solution)/shard_map/ppermute | solution.py:241
  34.8 0.9 %shard_map.107 = (f32[16,1280]{1,0:T(8,128)S(1)}, bf16[8,16,128]{2,1,0:T(8,128)(2,1)S(1)}) custom-call(s32[3]{0:T(128)S(1)} %pad_add_fusion.place_ref, s32[1,6]{1,0:T(1,128)S(1)} %bitcast.43, s32[6,1,128]{2,1,0:T(1,128)S(1)} %bitcast.39, f32[16,1280]{1,0:T(8,128)S(1)} %bitcast.32, f32[16,1280]{1,0:T(8,128)S(1)} %shard_map.106.y_ref, ...), custom_call_target="tpu_custom_call" | custom-call | tf_op jit(solution)/shard_map/pallas_call | solution.py:186
  35.6 7.2 %all_to_all.16.got_ref = bf16[8,16,128]{2,1,0:T(8,128)(2,1)S(1)} all-to-all(bf16[8,16,128]{2,1,0:T(8,128)(2,1)S(1)} %get-tuple-element.31), channel_id=1, replica_groups=mesh['sub'=8,'reg'=4] {'sub'}, dimensions={0} | all-to-all | bytes 65536 | tf_op jit(solution)/shard_map/all_to_all | solution.py:251
  42.9 1.1 %shard_map.108 = (f32[16,1280]{1,0:T(8,128)S(1)}, bf16[16,1280]{1,0:T(8,128)(2,1)S(1)}, bf16[1,16,128]{2,1,0:T(8,128)(2,1)S(1)}, bf16[2,16,128]{2,1,0:T(8,128)(2...) custom-call(s32[3]{0:T(128)S(1)} %pad_add_fusion.place_ref, s32[1,6]{1,0:T(1,128)S(1)} %bitcast.44, ...), custom_call_target="tpu_custom_call" | custom-call | tf_op jit(solution)/shard_map/pallas_call | solution.py:186
  44.0 1.6 %collective-permute-start.5 = (bf16[2,16,128]{2,1,0:T(8,128)(2,1)S(1)}, bf16[2,16,128]{2,1,0:T(8,128)(2,1)S(1)}, u32[]{:S(2)}, u32[]{:S(2)}) collective-permute-start(bf16[2,16,128]{2,1,0:T(8,128)(2,1)S(1)} %get-tuple-element.37), channel_id=1, source_target_pairs={{1,2},{2,1},{3,0},{0,3},{5,6},{6,5},{7,4},{4,7},{9,10},{10,9},{11,... | collective-permute-start | bytes 24584 | tf_op jit(solution)/shard_map/ppermute | solution.py:241
  46.8 2.0 %shard_map.109.y_ref = f32[16,1280]{1,0:T(8,128)S(1)} custom-call(s32[2,80]{1,0:T(2,128)S(1)} %bitcast.49, bf16[16,1280]{1,0:T(8,128)(2,1)S(1)} %get-tuple-element.35.x_ref, bf16[80,128,128]{2,1,0:T(8,128)(2,1)S(1)} %get-tuple-element.26.tiles_ref), custom_call_target="tpu_custom_call" | custom-call | tf_op jit(solution)/shard_map/pallas_call | solution.py:186
  48.8 1.2 %collective-permute-done.4.refs_0_ = bf16[1,16,128]{2,1,0:T(8,128)(2,1)S(1)} collective-permute-done((bf16[1,16,128]{2,1,0:T(8,128)(2,1)S(1)}, bf16[1,16,128]{2,1,0:T(8,128)(2,1)S(1)}, u32[]{:S(2)}, u32[]{:S(2)}) %collective-permute-start.4) | collective-permute-done | bytes 4128 | tf_op jit(solution)/shard_map/ppermute | solution.py:241
  50.1 0.9 %shard_map.110 = (f32[16,1280]{1,0:T(8,128)S(1)}, bf16[8,16,128]{2,1,0:T(8,128)(2,1)S(1)}) custom-call(s32[3]{0:T(128)S(1)} %pad_add_fusion.place_ref, s32[1,6]{1,0:T(1,128)S(1)} %bitcast.45, s32[6,1,128]{2,1,0:T(1,128)S(1)} %bitcast.40, f32[16,1280]{1,0:T(8,128)S(1)} %bitcast.33, f32[16,1280]{1,0:T(8,128)S(1)} %shard_map.109.y_ref, ...), custom_call_target="tpu_custom_call" | custom-call | tf_op jit(solution)/shard_map/pallas_call | solution.py:186
  51.0 7.2 %all_to_all.17.got_ref = bf16[8,16,128]{2,1,0:T(8,128)(2,1)S(1)} all-to-all(bf16[8,16,128]{2,1,0:T(8,128)(2,1)S(1)} %get-tuple-element.40), channel_id=1, replica_groups=mesh['sub'=8,'reg'=4] {'sub'}, dimensions={0} | all-to-all | bytes 65536 | tf_op jit(solution)/shard_map/all_to_all | solution.py:251
  58.2 1.7 %shard_map.111 = (f32[16,1280]{1,0:T(8,128)}, bf16[16,1280]{1,0:T(8,128)(2,1)S(1)}, bf16[1,16,128]{2,1,0:T(8,128)(2,1)S(1)}, bf16[2,16,128]{2,1,0:T(8,128)(2,1)S...) custom-call(s32[3]{0:T(128)S(1)} %pad_add_fusion.place_ref, s32[1,6]{1,0:T(1,128)S(1)} %bitcast.46, ...), custom_call_target="tpu_custom_call" | custom-call | tf_op jit(solution)/shard_map/pallas_call | solution.py:186
  59.9 2.8 %collective-permute-start.9 = (bf16[2,16,128]{2,1,0:T(8,128)(2,1)S(1)}, bf16[2,16,128]{2,1,0:T(8,128)(2,1)S(1)}, u32[]{:S(2)}, u32[]{:S(2)}) collective-permute-start(bf16[2,16,128]{2,1,0:T(8,128)(2,1)S(1)} %get-tuple-element.45), channel_id=1, source_target_pairs={{1,2},{2,1},{3,0},{0,3},{5,6},{6,5},{7,4},{4,7},{9,10},{10,9},{11,... | collective-permute-start | bytes 24584 | tf_op jit(solution)/shard_map/ppermute | solution.py:241
  63.5 2.0 %shard_map.112.y_ref = f32[16,1280]{1,0:T(8,128)S(1)} custom-call(s32[2,80]{1,0:T(2,128)S(1)} %bitcast.50, bf16[16,1280]{1,0:T(8,128)(2,1)S(1)} %get-tuple-element.43.x_ref, bf16[80,128,128]{2,1,0:T(8,128)(2,1)S(1)} %get-tuple-element.26.tiles_ref), custom_call_target="tpu_custom_call" | custom-call | tf_op jit(solution)/shard_map/pallas_call | solution.py:186
  66.7 1.4 %shard_map.113 = bf16[16,1280]{1,0:T(8,128)(2,1)} custom-call(s32[3]{0:T(128)S(1)} %pad_add_fusion.place_ref, s32[1,6]{1,0:T(1,128)S(1)} %bitcast.47, s32[6,1,128]{2,1,0:T(1,128)S(1)} %bitcast.41, f32[16,1280]{1,0:T(8,128)S(1)} %bitcast.34, f32[16,1280]{1,0:T(8,128)S(1)} %shard_map.112.y_ref, bf16[1,16,128]{2,1,0:T(8,128)(2,1)S(1)} %collective-permute-done.8.refs_0_, ...), custom_call_target="tpu_custom_call" | custom-call | tf_op jit(solution)/shard_map/pallas_call | solution.py:186
  (39 shorter events, 5.3 us)
Async XLA Ops:
  0.7 1.0 %copy-start = (bf16[1,1,1280,128]{3,2,1,0:T(8,128)(2,1)S(1)}, bf16[1,1,1280,128]{3,2,1,0:T(8,128)(2,1)}, u32[]{:S(2)}) copy-start(bf16[1,1,1280,128]{3,2,1,0:T(8,128)(2,1)} %param.15) | copy-start | bytes 983044
  1.7 0.9 %copy-start.3 = (f32[1,1,1280,16]{2,3,1,0:T(8,128)S(1)}, f32[1,1,1280,16]{2,3,1,0:T(8,128)}, u32[]{:S(2)}) copy-start(f32[1,1,1280,16]{2,3,1,0:T(8,128)} %param.9) | copy-start | bytes 245764
  2.6 0.9 %copy-start.4 = (f32[1,64,512]{2,1,0:T(8,128)S(1)}, f32[1,64,512]{2,1,0:T(8,128)}, u32[]{:S(2)}) copy-start(f32[1,64,512]{2,1,0:T(8,128)} %param.17) | copy-start | bytes 393220
  3.5 0.7 copy-start.10
  4.9 26.6 %copy-start.9 = (s32[1,1,80,2]{2,3,1,0:T(2,128)S(1)}, s32[1,1,80,2]{2,3,1,0:T(2,128)}, u32[]{:S(2)}) copy-start(s32[1,1,80,2]{2,3,1,0:T(2,128)} %param.11) | copy-start | bytes 1924
  20.4 1.7 %copy-start.2 = (bf16[1,1,80,128,128]{4,3,2,1,0:T(8,128)(2,1)S(1)}, bf16[1,1,80,128,128]{4,3,2,1,0:T(8,128)(2,1)}, u32[]{:S(2)}) copy-start(bf16[1,1,80,128,128]{4,3,2,1,0:T(8,128)(2,1)} %param.10) | copy-start | bytes 7864324
  22.1 0.7 %copy-start.5 = (f32[1,1,1280]{2,1,0:T(1,128)S(1)}, f32[1,1,1280]{2,1,0:T(1,128)}, u32[]{:S(2)}) copy-start(f32[1,1,1280]{2,1,0:T(1,128)} %param.12) | copy-start | bytes 15364
  22.8 0.7 copy-start.7
  23.5 0.7 copy-start.11
  24.1 10.6 %copy-start.6 = (s32[1,1,6,128]{3,1,2,0:T(1,128)S(1)}, s32[1,1,6,128]{3,1,2,0:T(1,128)}, u32[]{:S(2)}) copy-start(s32[1,1,6,128]{3,1,2,0:T(1,128)} %param.14) | copy-start | bytes 9220
  24.1 10.6 %copy-start.8 = (s32[1,1,6]{2,1,0:T(1,128)S(1)}, s32[1,1,6]{2,1,0:T(1,128)}, u32[]{:S(2)}) copy-start(s32[1,1,6]{2,1,0:T(1,128)} %param.13) | copy-start | bytes 76
  24.1 18.7 %copy-start.1 = (bf16[1,1,1280,128]{3,2,1,0:T(8,128)(2,1)S(1)}, bf16[1,1,1280,128]{3,2,1,0:T(8,128)(2,1)}, u32[]{:S(2)}) copy-start(bf16[1,1,1280,128]{3,2,1,0:T(8,128)(2,1)} %param.15) | copy-start | bytes 983044
  27.1 7.6 %collective-permute-start.1 = (bf16[2,16,128]{2,1,0:T(8,128)(2,1)S(1)}, bf16[2,16,128]{2,1,0:T(8,128)(2,1)S(1)}, u32[]{:S(2)}, u32[]{:S(2)}) collective-permute-start(bf16[2,16,128]{2,1,0:T(8,128)(2,1)S(1)} %get-tuple-element.28), channel_id=1, source_target_pairs={{1,2},{2,1},{3,0},{0,3},{5,6},{6,5},{7,4},{4,7},{9,10},{10,9},{11,... | collective-permute-start | bytes 24584 | tf_op jit(solution)/shard_map/ppermute | solution.py:241
  30.8 3.9 %collective-permute-start.2 = (bf16[2,16,128]{2,1,0:T(8,128)(2,1)S(1)}, bf16[2,16,128]{2,1,0:T(8,128)(2,1)S(1)}, u32[]{:S(2)}, u32[]{:S(2)}) collective-permute-start(bf16[2,16,128]{2,1,0:T(8,128)(2,1)S(1)} %get-tuple-element.29), channel_id=1, source_target_pairs={{0,1},{1,0},{2,3},{3,2},{4,5},{5,4},{6,7},{7,6},{8,9},{9,8},{10,11... | collective-permute-start | bytes 24584 | tf_op jit(solution)/shard_map/ppermute | solution.py:241
  30.8 3.9 %collective-permute-start = (bf16[1,16,128]{2,1,0:T(8,128)(2,1)S(1)}, bf16[1,16,128]{2,1,0:T(8,128)(2,1)S(1)}, u32[]{:S(2)}, u32[]{:S(2)}) collective-permute-start(bf16[1,16,128]{2,1,0:T(8,128)(2,1)S(1)} %get-tuple-element.27), channel_id=1, source_target_pairs={{4,8},{8,4},{12,16},{16,12},{20,24},{24,20},{28,0},{0,28},{5,9},{9... | collective-permute-start | bytes 12296 | tf_op jit(solution)/shard_map/ppermute | solution.py:241
  30.8 3.9 %collective-permute-start.3 = (bf16[1,16,128]{2,1,0:T(8,128)(2,1)S(1)}, bf16[1,16,128]{2,1,0:T(8,128)(2,1)S(1)}, u32[]{:S(2)}, u32[]{:S(2)}) collective-permute-start(bf16[1,16,128]{2,1,0:T(8,128)(2,1)S(1)} %get-tuple-element.30), channel_id=1, source_target_pairs={{0,4},{4,0},{8,12},{12,8},{16,20},{20,16},{24,28},{28,24},{1,5},{5... | collective-permute-start | bytes 12296 | tf_op jit(solution)/shard_map/ppermute | solution.py:241
  44.0 6.1 %collective-permute-start.5 = (bf16[2,16,128]{2,1,0:T(8,128)(2,1)S(1)}, bf16[2,16,128]{2,1,0:T(8,128)(2,1)S(1)}, u32[]{:S(2)}, u32[]{:S(2)}) collective-permute-start(bf16[2,16,128]{2,1,0:T(8,128)(2,1)S(1)} %get-tuple-element.37), channel_id=1, source_target_pairs={{1,2},{2,1},{3,0},{0,3},{5,6},{6,5},{7,4},{4,7},{9,10},{10,9},{11,... | collective-permute-start | bytes 24584 | tf_op jit(solution)/shard_map/ppermute | solution.py:241
  45.5 4.6 %collective-permute-start.6 = (bf16[2,16,128]{2,1,0:T(8,128)(2,1)S(1)}, bf16[2,16,128]{2,1,0:T(8,128)(2,1)S(1)}, u32[]{:S(2)}, u32[]{:S(2)}) collective-permute-start(bf16[2,16,128]{2,1,0:T(8,128)(2,1)S(1)} %get-tuple-element.38), channel_id=1, source_target_pairs={{0,1},{1,0},{2,3},{3,2},{4,5},{5,4},{6,7},{7,6},{8,9},{9,8},{10,11... | collective-permute-start | bytes 24584 | tf_op jit(solution)/shard_map/ppermute | solution.py:241
  46.2 3.9 %collective-permute-start.4 = (bf16[1,16,128]{2,1,0:T(8,128)(2,1)S(1)}, bf16[1,16,128]{2,1,0:T(8,128)(2,1)S(1)}, u32[]{:S(2)}, u32[]{:S(2)}) collective-permute-start(bf16[1,16,128]{2,1,0:T(8,128)(2,1)S(1)} %get-tuple-element.36), channel_id=1, source_target_pairs={{4,8},{8,4},{12,16},{16,12},{20,24},{24,20},{28,0},{0,28},{5,9},{9... | collective-permute-start | bytes 12296 | tf_op jit(solution)/shard_map/ppermute | solution.py:241
  46.2 3.9 %collective-permute-start.7 = (bf16[1,16,128]{2,1,0:T(8,128)(2,1)S(1)}, bf16[1,16,128]{2,1,0:T(8,128)(2,1)S(1)}, u32[]{:S(2)}, u32[]{:S(2)}) collective-permute-start(bf16[1,16,128]{2,1,0:T(8,128)(2,1)S(1)} %get-tuple-element.39), channel_id=1, source_target_pairs={{0,4},{4,0},{8,12},{12,8},{16,20},{20,16},{24,28},{28,24},{1,5},{5... | collective-permute-start | bytes 12296 | tf_op jit(solution)/shard_map/ppermute | solution.py:241
  59.9 6.8 %collective-permute-start.9 = (bf16[2,16,128]{2,1,0:T(8,128)(2,1)S(1)}, bf16[2,16,128]{2,1,0:T(8,128)(2,1)S(1)}, u32[]{:S(2)}, u32[]{:S(2)}) collective-permute-start(bf16[2,16,128]{2,1,0:T(8,128)(2,1)S(1)} %get-tuple-element.45), channel_id=1, source_target_pairs={{1,2},{2,1},{3,0},{0,3},{5,6},{6,5},{7,4},{4,7},{9,10},{10,9},{11,... | collective-permute-start | bytes 24584 | tf_op jit(solution)/shard_map/ppermute | solution.py:241
  62.8 3.9 %collective-permute-start.10 = (bf16[2,16,128]{2,1,0:T(8,128)(2,1)S(1)}, bf16[2,16,128]{2,1,0:T(8,128)(2,1)S(1)}, u32[]{:S(2)}, u32[]{:S(2)}) collective-permute-start(bf16[2,16,128]{2,1,0:T(8,128)(2,1)S(1)} %get-tuple-element.46), channel_id=1, source_target_pairs={{0,1},{1,0},{2,3},{3,2},{4,5},{5,4},{6,7},{7,6},{8,9},{9,8},{10,11... | collective-permute-start | bytes 24584 | tf_op jit(solution)/shard_map/ppermute | solution.py:241
  62.8 3.9 %collective-permute-start.8 = (bf16[1,16,128]{2,1,0:T(8,128)(2,1)S(1)}, bf16[1,16,128]{2,1,0:T(8,128)(2,1)S(1)}, u32[]{:S(2)}, u32[]{:S(2)}) collective-permute-start(bf16[1,16,128]{2,1,0:T(8,128)(2,1)S(1)} %get-tuple-element.44), channel_id=1, source_target_pairs={{4,8},{8,4},{12,16},{16,12},{20,24},{24,20},{28,0},{0,28},{5,9},{9... | collective-permute-start | bytes 12296 | tf_op jit(solution)/shard_map/ppermute | solution.py:241
  62.8 3.9 %collective-permute-start.11 = (bf16[1,16,128]{2,1,0:T(8,128)(2,1)S(1)}, bf16[1,16,128]{2,1,0:T(8,128)(2,1)S(1)}, u32[]{:S(2)}, u32[]{:S(2)}) collective-permute-start(bf16[1,16,128]{2,1,0:T(8,128)(2,1)S(1)} %get-tuple-element.47), channel_id=1, source_target_pairs={{0,4},{4,0},{8,12},{12,8},{16,20},{20,16},{24,28},{28,24},{1,5},{5... | collective-permute-start | bytes 12296 | tf_op jit(solution)/shard_map/ppermute | solution.py:241

commit v2 on v1

v2 whole, which is shorter than its diff:
```python
import functools

import jax
import jax.numpy as jnp
from jax import lax
from jax.experimental import pallas as pl
from jax.experimental.pallas import tpu as pltpu
from jax.sharding import PartitionSpec as P

SWEEPS = 3
F32 = jnp.float32
BF16 = jnp.bfloat16
I32 = jnp.int32
VMEM = pl.BlockSpec(memory_space=pltpu.VMEM)
FAR = pl.BlockSpec(memory_space=pltpu.HBM)
SMEM = pl.BlockSpec(memory_space=pltpu.SMEM)
NT = (((1,), (1,)), ((), ()))
NN = (((1,), (0,)), ((), ()))


def matmul(a, b, dims):
    return lax.dot_general(a, b, dims, preferred_element_type=F32)


def at_block(block, tile):
    return pl.ds(pl.multiple_of(block * tile, tile), tile)


def lanes(ref):
    return jnp.concatenate([ref[b] for b in range(ref.shape[0])], axis=1)


def one_hot(mask):
    return mask.astype(F32).astype(BF16)


def blocks_of(value, tile):
    return [value[:, at : at + tile] for at in range(0, value.shape[1], tile)]


def code_rows(parts):
    return -(-(2 + parts) // 16) * 16


def first_kernel(
    groups,
    place_ref,
    rhs_far,
    basis_far,
    inverse_far,
    weights_far,
    ids_far,
    faces_far,
    chunk_far,
    rhs_ref,
    basis_ref,
    weights_ref,
    ids_ref,
    masks_ref,
    inverse_ref,
    packed_ref,
    faces_ref,
    in_sems,
    out_sems,
):
    pairs = (
        (inverse_far, inverse_ref),
        (ids_far, ids_ref),
        (rhs_far, rhs_ref),
        (basis_far, basis_ref),
        (weights_far, weights_ref),
        (faces_far, faces_ref),
    )
    copies = [pltpu.make_async_copy(*pair, in_sems.at[n]) for n, pair in enumerate(pairs)]
    for copy in copies:
        copy.start()
    rights = rhs_ref.shape[0]
    held, total = inverse_ref.shape
    count = ids_ref.shape[1]
    parts = total // count
    head = code_rows(parts)
    copies[0].wait()
    copies[1].wait()
    ids = ids_ref[...]
    on_diagonal = lax.broadcasted_iota(I32, (held, total), 1) == (
        lax.broadcasted_iota(I32, (held, total), 0) + place_ref[0] * held
    )
    inverse = inverse_ref[...]
    rounded = inverse.astype(BF16)
    dropped = jnp.where(on_diagonal, inverse - rounded.astype(F32), 0.0)
    dropped = jnp.sum(dropped, axis=0, keepdims=True)
    codes = [(ids // 128).astype(F32), (ids % 128).astype(F32)] + blocks_of(dropped, count)
    row = lax.broadcasted_iota(I32, (head, count), 0)
    coded = jnp.zeros((head, count), F32)
    for n, code in enumerate(codes):
        coded = jnp.where(row == n, code, coded)
    packed_ref[:head] = coded.astype(BF16)
    for q, piece in enumerate(blocks_of(rounded, count)):
        at = head + rights + q * held
        packed_ref[at : at + held] = piece
    copies[2].wait()
    copies[3].wait()
    packed_ref[head : head + rights] = matmul(rhs_ref[...].astype(BF16), basis_ref[...], NN).astype(BF16)
    outs = [
        pltpu.make_async_copy(packed_ref, chunk_far.at[i], out_sems.at[i])
        for i in range(chunk_far.shape[0])
    ]
    for copy in outs:
        copy.start()
    copies[4].wait()
    copies[5].wait()
    flat = [(face, turn) for faces, turn in groups for face in faces]
    block = lax.broadcasted_iota(I32, masks_ref.shape[1:], 0)
    for n, (face, turn) in enumerate(flat):
        masks_ref[n] = (block == faces_ref[0, face ^ place_ref[turn]]).astype(F32)
    for copy in outs:
        copy.wait()


def update(z, basis_ref, weights_ref, u, r, masks_ref, new_ref, out_refs):
    tile = out_refs[0].shape[2]
    value = weights_ref[...] * r + matmul(z.astype(BF16), basis_ref[...], NT)
    if u is not None:
        value = u + value
    new_ref[...] = value
    blocks = blocks_of(value, tile)
    at = 0
    for out_ref in out_refs:
        for n in range(out_ref.shape[0]):
            face = sum(masks_ref[at, b : b + 1] * block for b, block in enumerate(blocks))
            out_ref[n] = face.astype(BF16)
            at += 1


def opening_kernel(total, ids_ref, got_ref, basis_ref, weights_ref, r_ref, masks_ref, block_ref, new_ref, *out_refs):
    peers = got_ref.shape[0]
    rights = r_ref.shape[0]
    count = ids_ref.shape[1]
    parts = total // count
    head = code_rows(parts)
    body_at = head + rights
    held = (got_ref.shape[1] - body_at) // parts
    codes = [got_ref[i, :head, :].astype(F32) for i in range(peers)]
    dropped = sum(codes)
    column = jnp.broadcast_to(ids_ref[...].astype(F32), (count, count)).T
    lane = lax.broadcasted_iota(I32, (count, count), 1).astype(F32)
    own = [column == lane + float(q * count) for q in range(parts)]
    own_low = jnp.concatenate([one_hot(hot) for hot in own], axis=1)
    own_rows, own_dropped = [], []
    for q in range(parts):
        piece = got_ref[:, body_at + q * held : body_at + (q + 1) * held, :].reshape(peers * held, count)
        own_rows.append(matmul(own_low, piece, NN).astype(BF16))
        own_dropped.append(jnp.where(own[q], dropped[2 + q : 3 + q], 0.0).astype(BF16))
    own_rows = jnp.concatenate(
        [jnp.concatenate(own_rows, axis=1), jnp.concatenate(own_dropped, axis=1)], axis=0
    )
    index = lax.broadcasted_iota(I32, (total, count), 0).astype(F32)
    z = jnp.zeros((rights, count), F32)
    for i in range(peers):
        ids = codes[i][0:1] * 128.0 + codes[i][1:2]
        piece = matmul(own_rows, one_hot(index == ids), NN).astype(BF16)
        block_ref[i] = piece
        both = matmul(got_ref[i, head:body_at, :], piece, NT)
        z = z + both[:, :count] + both[:, count:]
    update(z, basis_ref, weights_ref, None, r_ref[...], masks_ref, new_ref, out_refs)


def correct_kernel(got_ref, block_ref, basis_ref, weights_ref, u_ref, r_ref, masks_ref, new_ref, *out_refs):
    count = got_ref.shape[2]
    both = matmul(lanes(got_ref), lanes(block_ref), NT)
    z = both[:, :count] + both[:, count:]
    update(z, basis_ref, weights_ref, u_ref[...], r_ref[...], masks_ref, new_ref, out_refs)


def subtract_tile(t, list_ref, low_ref, tile_ref, rhs_ref, base_ref):
    tile = tile_ref.shape[0]
    product = matmul(low_ref[:, at_block(list_ref[1, t], tile)], tile_ref[...], NT)
    if t * tile < base_ref.shape[1]:
        cut = slice(t * tile, (t + 1) * tile)
        base_ref[:, cut] = rhs_ref[:, cut] - product
    else:
        cut = at_block(list_ref[0, t], tile)
        base_ref[:, cut] = base_ref[:, cut] - product


def local_kernel(list_ref, u_ref, tiles_ref, rhs_ref, base_ref, low_ref):
    low_ref[...] = u_ref[...].astype(BF16)
    for t in range(tiles_ref.shape[0]):
        subtract_tile(t, list_ref, low_ref, tiles_ref.at[t], rhs_ref, base_ref)


def local_first_kernel(groups, list_ref, place_ref, u_ref, tiles_ref, rhs_ref, match_ref, base_ref, low_ref, tables_ref):
    flat = [(face, turn) for faces, turn in groups for face in faces]
    index = lax.broadcasted_iota(I32, tables_ref.shape[1:], 0)
    for n, (face, turn) in enumerate(flat):
        tables_ref[n] = one_hot(index == match_ref[face ^ place_ref[turn]])
    local_kernel(list_ref, u_ref, tiles_ref, rhs_ref, base_ref, low_ref)


def coupled(tables_ref, masks_ref, base_ref, in_refs):
    got = []
    for in_ref in in_refs:
        for n in range(in_ref.shape[0]):
            got.append(0.5 * matmul(in_ref[n], tables_ref[len(got)], NN))
    blocks = blocks_of(base_ref[...], got[0].shape[1])
    return jnp.concatenate(
        [
            block + sum(masks_ref[n, b : b + 1] * face for n, face in enumerate(got))
            for b, block in enumerate(blocks)
        ],
        axis=1,
    )


def residual_kernel(tables_ref, masks_ref, base_ref, basis_ref, *refs):
    *in_refs, r_ref, chunk_ref = refs
    residual = coupled(tables_ref, masks_ref, base_ref, in_refs)
    r_ref[...] = residual
    coarse = matmul(residual.astype(BF16), basis_ref[...], NN).astype(BF16)
    for i in range(chunk_ref.shape[0]):
        chunk_ref[i] = coarse


def last_kernel(tables_ref, masks_ref, base_ref, *refs):
    *in_refs, out_ref = refs
    out_ref[...] = coupled(tables_ref, masks_ref, base_ref, in_refs).astype(BF16)


def call(kernel, outs, args, scalars=0, far_args=0, far_outs=0, scratch=()):
    return pl.pallas_call(
        kernel,
        out_shape=outs,
        in_specs=[SMEM] * scalars + [FAR] * far_args + [VMEM] * (len(args) - scalars - far_args),
        out_specs=[FAR] * far_outs + [VMEM] * (len(outs) - far_outs),
        scratch_shapes=list(scratch),
        compiler_params=pltpu.CompilerParams(vmem_limit_bytes=16 << 20),
    )(*args)


def far(array):
    return pltpu.with_memory_space_constraint(array, pltpu.HBM)


def near(array):
    return pltpu.with_memory_space_constraint(array, pltpu.VMEM)


def body(
    right_side,
    tiles,
    tile_list,
    weights,
    face_map,
    matching,
    coarse_basis,
    coarse_map,
    coarse_inverse,
):
    order, rights = right_side.shape[2:]
    tile = tiles.shape[3]
    listing = tile_list[0, 0].T
    count = coarse_map.shape[2]
    inverse_rows = coarse_inverse[0]
    held, total = inverse_rows.shape
    peers = lax.axis_size("sub")
    stride = max(lax.axis_size("reg") // 4, 1)
    place = jnp.stack(
        [lax.axis_index("sub"), lax.axis_index("sub") % 2]
        + [lax.axis_index("reg") // far % 2 for far in sorted({1, stride})]
    ).astype(I32)
    if stride == 1:
        swaps = (((0, 2), "reg", 1, False, 2), ((1, 3), "reg", 1, True, 2))
    else:
        swaps = (
            ((0,), "reg", 1, False, 2),
            ((2,), "reg", stride, False, 3),
            ((1,), "reg", 1, True, 2),
            ((3,), "reg", stride, True, 3),
        )
    swaps = ((((4,), "sub", 1, False, 1),) + swaps + (((5,), "sub", 1, True, 1),))
    groups = tuple((faces, turn) for faces, _, _, _, turn in swaps)

    def swap(shard, axis, far, ahead):
        n = lax.axis_size(axis)
        assert n // far % 2 == 0
        pairs = []
        for i in range(n):
            if (i // far % 2 == 0) == ahead:
                pairs += [(i, (i + far) % n), ((i + far) % n, i)]
        return lax.ppermute(shard, axis, pairs)

    near_out, far_out = pltpu.VMEM, jax.ShapeDtypeStruct
    field = near_out((rights, order), F32)
    face_outs = [far_out((len(faces), rights, tile), BF16) for faces, _ in groups]
    face_count = sum(len(faces) for faces, _ in groups)
    parts = total // count
    rows = code_rows(parts) + rights + held * parts

    def spread(chunk):
        return near(lax.all_to_all(chunk, "sub", split_axis=0, concat_axis=0, tiled=True))

    chunk, rhs, basis, scaling, ids, masks = call(
        functools.partial(first_kernel, groups),
        [
            far_out((peers, rows, count), BF16),
            field,
            near_out((order, count), BF16),
            near_out((1, order), F32),
            near_out((1, count), I32),
            near_out((face_count, -(-(order // tile) // 8) * 8, tile), F32),
        ],
        [
            place,
            far(right_side[0, 0].T),
            far(coarse_basis[0, 0]),
            far(inverse_rows),
            far(weights[0]),
            far(coarse_map[0]),
            far(face_map[0]),
        ],
        scalars=1,
        far_args=6,
        far_outs=1,
        scratch=[
            pltpu.VMEM((held, total), F32),
            pltpu.VMEM((rows, count), BF16),
            pltpu.SMEM(face_map.shape[1:], I32),
            pltpu.SemaphoreType.DMA((6,)),
            pltpu.SemaphoreType.DMA((peers,)),
        ],
    )
    tile_block = tiles[0, 0]
    residual = rhs
    for sweep in range(SWEEPS):
        got = spread(chunk)
        if sweep == 0:
            block, u, *faces = call(
                functools.partial(opening_kernel, total),
                [near_out((peers, 2 * count, count), BF16), field, *face_outs],
                [ids, got, basis, scaling, residual, masks],
            )
        else:
            u, *faces = call(
                correct_kernel, [field, *face_outs], [got, block, basis, scaling, u, residual, masks]
            )
        arrived = [near(swap(face, *how[1:4])) for face, how in zip(faces, swaps, strict=True)]
        low_out = (near_out if sweep + 1 < SWEEPS else far_out)((rights, order), BF16)
        if sweep == 0:
            base, low, tables = call(
                functools.partial(local_first_kernel, groups),
                [field, low_out, near_out((face_count, tile, tile), BF16)],
                [listing, place, u, tile_block, rhs, matching[0].reshape(-1, 1, tile)],
                scalars=2,
            )
        else:
            base, low = call(local_kernel, [field, low_out], [listing, u, tile_block, rhs], scalars=1)
        if sweep + 1 < SWEEPS:
            residual, chunk = call(
                residual_kernel,
                [field, far_out((peers, rights, count), BF16)],
                [tables, masks, base, basis, *arrived],
            )
        else:
            (left,) = call(
                last_kernel, [far_out((rights, order), BF16)], [tables, masks, base, *arrived]
            )
    return low.T[None, None], left.T[None, None]


def solution(mesh):
    placed = (
        P("sub", "reg", None, None),
        P("sub", "reg", None, None, None),
        P("sub", "reg", None, None),
        P("sub", "reg", None),
        P("sub", "reg", None),
        P("sub", "reg", None, None),
        P("sub", "reg", None, None),
        P("sub", "reg", None),
        P("reg", "sub", None),
    )
    return jax.shard_map(
        body,
        mesh=mesh,
        in_specs=placed,
        out_specs=(P("sub", "reg", None, None), P("sub", "reg", None, None)),
        check_vma=False,
    )
```

time: 68.5 us -> 59.8 us (0.87)
  local copies, waits for them, and re-layouts: 7.81 us -> 0.01 us
  waiting for transfers between devices: 3.1 us -> 2.21 us
    unnamed x25 -> x6, local copies, waits for them, and re-layouts: 7.81 us -> 0.01 us
    ppermute x12, waiting for transfers between devices: 3.1 us -> 2.21 us  [swap(): return lax.ppermute(shard, axis, pairs)]
  transfers between devices with their start and end apart: 12 -> 12, of which waited for: 3 -> 3; matrix products, arithmetic and copies ran while one was open for 1% -> 0% of each run, Pallas kernels for 9% -> 13%
where the time goes in v2:
time: 59.8 us; the launch traced here: 59.6 us
  blocking collectives  30.5 us (51%)
  Pallas kernels  15.2 us (25%)
  starting transfers between devices  10.8 us (18%)
  waiting for transfers between devices  2.21 us (4%)
  between operations  0.75 us (1%)
    all_to_all x3, blocking collectives, spread(): lax.all_to_all(chunk, 'sub', split_axis=0, concat_axis=0, tiled=True)  30.5 us
    pallas_call x10, Pallas kernels, call(): pl.pallas_call(kernel, out_shape=outs, in_specs=[SMEM] * scalars + [FAR]...  15.2 us
    ppermute x12, starting transfers between devices, swap(): return lax.ppermute(shard, axis, pairs)  10.8 us
    ppermute x12, waiting for transfers between devices, swap(): return lax.ppermute(shard, axis, pairs)  2.21 us
  transfers between devices with their start and end apart: 12, of which 3 were waited for; matrix products, arithmetic and copies ran while one was open for 0% of the time, Pallas kernels for 13%

profile of v2, /device:TPU:0, one launch (start us, length us, event | category | flops | bytes accessed | tf_op | source)
XLA Modules:
  0.0 59.6 jit_solution(4562626916667186511)
XLA Ops:
  0.7 0.1 pad_add_fusion.place_ref
  0.8 2.9 %shard_map.104 = (bf16[8,288,128]{2,1,0:T(8,128)(2,1)S(1)}, f32[16,1280]{1,0:T(8,128)S(1)}, bf16[1280,128]{1,0:T(8,128)(2,1)S(1)}, f32[1,1280]{1,0:T(1,128)S(1)}...) custom-call(s32[3]{0:T(128)S(1)} %pad_add_fusion.place_ref, f32[16,1280]{1,0:T(8,128)} %bitcast.31, ...), custom_call_target="tpu_custom_call" | custom-call | tf_op jit(solution)/shard_map/pallas_call | solution.py:230
  3.6 15.4 %all_to_all.15.got_ref = bf16[8,288,128]{2,1,0:T(8,128)(2,1)S(1)} all-to-all(bf16[8,288,128]{2,1,0:T(8,128)(2,1)S(1)} %get-tuple-element.34), channel_id=1, replica_groups=mesh['sub'=8,'reg'=4] {'sub'}, dimensions={0} | all-to-all | bytes 1179648 | tf_op jit(solution)/shard_map/all_to_all | solution.py:300
  19.0 2.2 %shard_map.105 = (bf16[8,256,128]{2,1,0:T(8,128)(2,1)S(1)}, f32[16,1280]{1,0:T(8,128)S(1)}, bf16[1,16,128]{2,1,0:T(8,128)(2,1)S(1)}, bf16[2,16,128]{2,1,0:T(8,12...) custom-call(s32[1,128]{1,0:T(1,128)S(1)} %get-tuple-element.33.ids_ref, ...), custom_call_target="tpu_custom_call" | custom-call | tf_op jit(solution)/shard_map/pallas_call | solution.py:230
  21.3 3.7 %collective-permute-start.1 = (bf16[2,16,128]{2,1,0:T(8,128)(2,1)S(1)}, bf16[2,16,128]{2,1,0:T(8,128)(2,1)S(1)}, u32[]{:S(2)}, u32[]{:S(2)}) collective-permute-start(bf16[2,16,128]{2,1,0:T(8,128)(2,1)S(1)} %get-tuple-element.43), channel_id=1, source_target_pairs={{1,2},{2,1},{3,0},{0,3},{5,6},{6,5},{7,4},{4,7},{9,10},{10,9},{11,... | collective-permute-start | bytes 24584 | tf_op jit(solution)/shard_map/ppermute | solution.py:290
  24.9 0.7 %collective-permute-start.3 = (bf16[1,16,128]{2,1,0:T(8,128)(2,1)S(1)}, bf16[1,16,128]{2,1,0:T(8,128)(2,1)S(1)}, u32[]{:S(2)}, u32[]{:S(2)}) collective-permute-start(bf16[1,16,128]{2,1,0:T(8,128)(2,1)S(1)} %get-tuple-element.45), channel_id=1, source_target_pairs={{0,4},{4,0},{8,12},{12,8},{16,20},{20,16},{24,28},{28,24},{1,5},{5... | collective-permute-start | bytes 12296 | tf_op jit(solution)/shard_map/ppermute | solution.py:290
  25.6 2.5 %shard_map.106 = (f32[16,1280]{1,0:T(8,128)S(1)}, bf16[16,1280]{1,0:T(8,128)(2,1)}, bf16[6,128,128]{2,1,0:T(8,128)(2,1)S(1)}) custom-call(s32[2,80]{1,0:T(2,128)S(1)} %bitcast.25, s32[3]{0:T(128)S(1)} %pad_add_fusion.place_ref, f32[16,1280]{1,0:T(8,128)S(1)} %get-tuple-element.39.u_ref, bf16[80,128,128]{2,1,0:T(8,128)(2,1)S(1)} %bitcast.22, ...), custom_call_target="tpu_custom_call" | custom-call | tf_op jit(solution)/shard_map/pallas_call | solution.py:230
  28.1 0.7 %collective-permute-done.refs_0_ = bf16[1,16,128]{2,1,0:T(8,128)(2,1)S(1)} collective-permute-done((bf16[1,16,128]{2,1,0:T(8,128)(2,1)S(1)}, bf16[1,16,128]{2,1,0:T(8,128)(2,1)S(1)}, u32[]{:S(2)}, u32[]{:S(2)}) %collective-permute-start) | collective-permute-done | bytes 4128 | tf_op jit(solution)/shard_map/ppermute | solution.py:290
  28.9 0.3 shard_map.107
  29.2 7.6 %all_to_all.16.got_ref = bf16[8,16,128]{2,1,0:T(8,128)(2,1)S(1)} all-to-all(bf16[8,16,128]{2,1,0:T(8,128)(2,1)S(1)} %get-tuple-element.46), channel_id=1, replica_groups=mesh['sub'=8,'reg'=4] {'sub'}, dimensions={0} | all-to-all | bytes 65536 | tf_op jit(solution)/shard_map/all_to_all | solution.py:300
  36.8 0.6 shard_map.108
  37.4 1.2 %collective-permute-start.5 = (bf16[2,16,128]{2,1,0:T(8,128)(2,1)S(1)}, bf16[2,16,128]{2,1,0:T(8,128)(2,1)S(1)}, u32[]{:S(2)}, u32[]{:S(2)}) collective-permute-start(bf16[2,16,128]{2,1,0:T(8,128)(2,1)S(1)} %get-tuple-element.52), channel_id=1, source_target_pairs={{1,2},{2,1},{3,0},{0,3},{5,6},{6,5},{7,4},{4,7},{9,10},{10,9},{11,... | collective-permute-start | bytes 24584 | tf_op jit(solution)/shard_map/ppermute | solution.py:290
  38.6 1.0 %collective-permute-start.6 = (bf16[2,16,128]{2,1,0:T(8,128)(2,1)S(1)}, bf16[2,16,128]{2,1,0:T(8,128)(2,1)S(1)}, u32[]{:S(2)}, u32[]{:S(2)}) collective-permute-start(bf16[2,16,128]{2,1,0:T(8,128)(2,1)S(1)} %get-tuple-element.53), channel_id=1, source_target_pairs={{0,1},{1,0},{2,3},{3,2},{4,5},{5,4},{6,7},{7,6},{8,9},{9,8},{10,11... | collective-permute-start | bytes 24584 | tf_op jit(solution)/shard_map/ppermute | solution.py:290
  39.5 0.7 %collective-permute-start.7 = (bf16[1,16,128]{2,1,0:T(8,128)(2,1)S(1)}, bf16[1,16,128]{2,1,0:T(8,128)(2,1)S(1)}, u32[]{:S(2)}, u32[]{:S(2)}) collective-permute-start(bf16[1,16,128]{2,1,0:T(8,128)(2,1)S(1)} %get-tuple-element.54), channel_id=1, source_target_pairs={{0,4},{4,0},{8,12},{12,8},{16,20},{20,16},{24,28},{28,24},{1,5},{5... | collective-permute-start | bytes 12296 | tf_op jit(solution)/shard_map/ppermute | solution.py:290
  40.2 2.5 %shard_map.109 = (f32[16,1280]{1,0:T(8,128)S(1)}, bf16[16,1280]{1,0:T(8,128)(2,1)}) custom-call(s32[2,80]{1,0:T(2,128)S(1)} %bitcast.26, f32[16,1280]{1,0:T(8,128)S(1)} %get-tuple-element.49.u_ref, bf16[80,128,128]{2,1,0:T(8,128)(2,1)S(1)} %bitcast.23, f32[16,1280]{1,0:T(8,128)S(1)} %get-tuple-element.37.r_ref.rhs_ref), custom_call_target="tpu_custom_call" | custom-call | tf_op jit(solution)/shard_map/pallas_call | solution.py:230
  42.7 0.7 %collective-permute-done.4.refs_0_ = bf16[1,16,128]{2,1,0:T(8,128)(2,1)S(1)} collective-permute-done((bf16[1,16,128]{2,1,0:T(8,128)(2,1)S(1)}, bf16[1,16,128]{2,1,0:T(8,128)(2,1)S(1)}, u32[]{:S(2)}, u32[]{:S(2)}) %collective-permute-start.4) | collective-permute-done | bytes 4128 | tf_op jit(solution)/shard_map/ppermute | solution.py:290
  43.5 0.3 shard_map.110
  43.8 7.5 %all_to_all.17.got_ref = bf16[8,16,128]{2,1,0:T(8,128)(2,1)S(1)} all-to-all(bf16[8,16,128]{2,1,0:T(8,128)(2,1)S(1)} %get-tuple-element.55), channel_id=1, replica_groups=mesh['sub'=8,'reg'=4] {'sub'}, dimensions={0} | all-to-all | bytes 65536 | tf_op jit(solution)/shard_map/all_to_all | solution.py:300
  51.3 0.6 shard_map.111
  51.9 2.9 %collective-permute-start.9 = (bf16[2,16,128]{2,1,0:T(8,128)(2,1)S(1)}, bf16[2,16,128]{2,1,0:T(8,128)(2,1)S(1)}, u32[]{:S(2)}, u32[]{:S(2)}) collective-permute-start(bf16[2,16,128]{2,1,0:T(8,128)(2,1)S(1)} %get-tuple-element.61), channel_id=1, source_target_pairs={{1,2},{2,1},{3,0},{0,3},{5,6},{6,5},{7,4},{4,7},{9,10},{10,9},{11,... | collective-permute-start | bytes 24584 | tf_op jit(solution)/shard_map/ppermute | solution.py:290
  54.9 0.7 %collective-permute-start.11 = (bf16[1,16,128]{2,1,0:T(8,128)(2,1)S(1)}, bf16[1,16,128]{2,1,0:T(8,128)(2,1)S(1)}, u32[]{:S(2)}, u32[]{:S(2)}) collective-permute-start(bf16[1,16,128]{2,1,0:T(8,128)(2,1)S(1)} %get-tuple-element.63), channel_id=1, source_target_pairs={{0,4},{4,0},{8,12},{12,8},{16,20},{20,16},{24,28},{28,24},{1,5},{5... | collective-permute-start | bytes 12296 | tf_op jit(solution)/shard_map/ppermute | solution.py:290
  55.5 2.5 %shard_map.112 = (f32[16,1280]{1,0:T(8,128)S(1)}, bf16[16,1280]{1,0:T(8,128)(2,1)}) custom-call(s32[2,80]{1,0:T(2,128)S(1)} %bitcast.27, f32[16,1280]{1,0:T(8,128)S(1)} %get-tuple-element.57.u_ref, bf16[80,128,128]{2,1,0:T(8,128)(2,1)S(1)} %bitcast.24, f32[16,1280]{1,0:T(8,128)S(1)} %get-tuple-element.37.r_ref.rhs_ref), custom_call_target="tpu_custom_call" | custom-call | tf_op jit(solution)/shard_map/pallas_call | solution.py:230
  58.1 0.7 %collective-permute-done.8.refs_0_ = bf16[1,16,128]{2,1,0:T(8,128)(2,1)S(1)} collective-permute-done((bf16[1,16,128]{2,1,0:T(8,128)(2,1)S(1)}, bf16[1,16,128]{2,1,0:T(8,128)(2,1)S(1)}, u32[]{:S(2)}, u32[]{:S(2)}) %collective-permute-start.8) | collective-permute-done | bytes 4128 | tf_op jit(solution)/shard_map/ppermute | solution.py:290
  58.8 0.8 %shard_map.113 = bf16[16,1280]{1,0:T(8,128)(2,1)} custom-call(bf16[6,128,128]{2,1,0:T(8,128)(2,1)S(1)} %get-tuple-element.40.tables_ref, f32[6,16,128]{2,1,0:T(8,128)S(1)} %get-tuple-element.38.masks_ref, f32[16,1280]{1,0:T(8,128)S(1)} %get-tuple-element.59.base_ref, bf16[1,16,128]{2,1,0:T(8,128)(2,1)S(1)} %collective-permute-done.8.refs_0_, ...), custom_call_target="tpu_custom_call" | custom-call | tf_op jit(solution)/shard_map/pallas_call | solution.py:230
  (20 shorter events, 0.0 us)
Async XLA Ops:
  0.6 25.0 %copy-start.2 = (s32[1,1,6,128]{3,1,2,0:T(1,128)S(1)}, s32[1,1,6,128]{3,1,2,0:T(1,128)}, u32[]{:S(2)}) copy-start(s32[1,1,6,128]{3,1,2,0:T(1,128)} %param.14) | copy-start | bytes 9220
  0.6 25.0 %copy-start.1 = (s32[1,1,80,2]{2,3,1,0:T(2,128)S(1)}, s32[1,1,80,2]{2,3,1,0:T(2,128)}, u32[]{:S(2)}) copy-start(s32[1,1,80,2]{2,3,1,0:T(2,128)} %param.11) | copy-start | bytes 1924
  0.7 25.0 %copy-start = (bf16[1,1,80,128,128]{4,3,2,1,0:T(8,128)(2,1)S(1)}, bf16[1,1,80,128,128]{4,3,2,1,0:T(8,128)(2,1)}, u32[]{:S(2)}) copy-start(bf16[1,1,80,128,128]{4,3,2,1,0:T(8,128)(2,1)} %param.10) | copy-start | bytes 7864324
  21.3 7.6 %collective-permute-start.1 = (bf16[2,16,128]{2,1,0:T(8,128)(2,1)S(1)}, bf16[2,16,128]{2,1,0:T(8,128)(2,1)S(1)}, u32[]{:S(2)}, u32[]{:S(2)}) collective-permute-start(bf16[2,16,128]{2,1,0:T(8,128)(2,1)S(1)} %get-tuple-element.43), channel_id=1, source_target_pairs={{1,2},{2,1},{3,0},{0,3},{5,6},{6,5},{7,4},{4,7},{9,10},{10,9},{11,... | collective-permute-start | bytes 24584 | tf_op jit(solution)/shard_map/ppermute | solution.py:290
  24.9 3.9 %collective-permute-start.2 = (bf16[2,16,128]{2,1,0:T(8,128)(2,1)S(1)}, bf16[2,16,128]{2,1,0:T(8,128)(2,1)S(1)}, u32[]{:S(2)}, u32[]{:S(2)}) collective-permute-start(bf16[2,16,128]{2,1,0:T(8,128)(2,1)S(1)} %get-tuple-element.44), channel_id=1, source_target_pairs={{0,1},{1,0},{2,3},{3,2},{4,5},{5,4},{6,7},{7,6},{8,9},{9,8},{10,11... | collective-permute-start | bytes 24584 | tf_op jit(solution)/shard_map/ppermute | solution.py:290
  24.9 3.9 %collective-permute-start = (bf16[1,16,128]{2,1,0:T(8,128)(2,1)S(1)}, bf16[1,16,128]{2,1,0:T(8,128)(2,1)S(1)}, u32[]{:S(2)}, u32[]{:S(2)}) collective-permute-start(bf16[1,16,128]{2,1,0:T(8,128)(2,1)S(1)} %get-tuple-element.42), channel_id=1, source_target_pairs={{4,8},{8,4},{12,16},{16,12},{20,24},{24,20},{28,0},{0,28},{5,9},{9... | collective-permute-start | bytes 12296 | tf_op jit(solution)/shard_map/ppermute | solution.py:290
  24.9 3.9 %collective-permute-start.3 = (bf16[1,16,128]{2,1,0:T(8,128)(2,1)S(1)}, bf16[1,16,128]{2,1,0:T(8,128)(2,1)S(1)}, u32[]{:S(2)}, u32[]{:S(2)}) collective-permute-start(bf16[1,16,128]{2,1,0:T(8,128)(2,1)S(1)} %get-tuple-element.45), channel_id=1, source_target_pairs={{0,4},{4,0},{8,12},{12,8},{16,20},{20,16},{24,28},{28,24},{1,5},{5... | collective-permute-start | bytes 12296 | tf_op jit(solution)/shard_map/ppermute | solution.py:290
  37.4 6.1 %collective-permute-start.5 = (bf16[2,16,128]{2,1,0:T(8,128)(2,1)S(1)}, bf16[2,16,128]{2,1,0:T(8,128)(2,1)S(1)}, u32[]{:S(2)}, u32[]{:S(2)}) collective-permute-start(bf16[2,16,128]{2,1,0:T(8,128)(2,1)S(1)} %get-tuple-element.52), channel_id=1, source_target_pairs={{1,2},{2,1},{3,0},{0,3},{5,6},{6,5},{7,4},{4,7},{9,10},{10,9},{11,... | collective-permute-start | bytes 24584 | tf_op jit(solution)/shard_map/ppermute | solution.py:290
  38.6 4.9 %collective-permute-start.6 = (bf16[2,16,128]{2,1,0:T(8,128)(2,1)S(1)}, bf16[2,16,128]{2,1,0:T(8,128)(2,1)S(1)}, u32[]{:S(2)}, u32[]{:S(2)}) collective-permute-start(bf16[2,16,128]{2,1,0:T(8,128)(2,1)S(1)} %get-tuple-element.53), channel_id=1, source_target_pairs={{0,1},{1,0},{2,3},{3,2},{4,5},{5,4},{6,7},{7,6},{8,9},{9,8},{10,11... | collective-permute-start | bytes 24584 | tf_op jit(solution)/shard_map/ppermute | solution.py:290
  39.5 3.9 %collective-permute-start.4 = (bf16[1,16,128]{2,1,0:T(8,128)(2,1)S(1)}, bf16[1,16,128]{2,1,0:T(8,128)(2,1)S(1)}, u32[]{:S(2)}, u32[]{:S(2)}) collective-permute-start(bf16[1,16,128]{2,1,0:T(8,128)(2,1)S(1)} %get-tuple-element.51), channel_id=1, source_target_pairs={{4,8},{8,4},{12,16},{16,12},{20,24},{24,20},{28,0},{0,28},{5,9},{9... | collective-permute-start | bytes 12296 | tf_op jit(solution)/shard_map/ppermute | solution.py:290
  39.5 3.9 %collective-permute-start.7 = (bf16[1,16,128]{2,1,0:T(8,128)(2,1)S(1)}, bf16[1,16,128]{2,1,0:T(8,128)(2,1)S(1)}, u32[]{:S(2)}, u32[]{:S(2)}) collective-permute-start(bf16[1,16,128]{2,1,0:T(8,128)(2,1)S(1)} %get-tuple-element.54), channel_id=1, source_target_pairs={{0,4},{4,0},{8,12},{12,8},{16,20},{20,16},{24,28},{28,24},{1,5},{5... | collective-permute-start | bytes 12296 | tf_op jit(solution)/shard_map/ppermute | solution.py:290
  51.9 6.9 %collective-permute-start.9 = (bf16[2,16,128]{2,1,0:T(8,128)(2,1)S(1)}, bf16[2,16,128]{2,1,0:T(8,128)(2,1)S(1)}, u32[]{:S(2)}, u32[]{:S(2)}) collective-permute-start(bf16[2,16,128]{2,1,0:T(8,128)(2,1)S(1)} %get-tuple-element.61), channel_id=1, source_target_pairs={{1,2},{2,1},{3,0},{0,3},{5,6},{6,5},{7,4},{4,7},{9,10},{10,9},{11,... | collective-permute-start | bytes 24584 | tf_op jit(solution)/shard_map/ppermute | solution.py:290
  54.9 3.9 %collective-permute-start.10 = (bf16[2,16,128]{2,1,0:T(8,128)(2,1)S(1)}, bf16[2,16,128]{2,1,0:T(8,128)(2,1)S(1)}, u32[]{:S(2)}, u32[]{:S(2)}) collective-permute-start(bf16[2,16,128]{2,1,0:T(8,128)(2,1)S(1)} %get-tuple-element.62), channel_id=1, source_target_pairs={{0,1},{1,0},{2,3},{3,2},{4,5},{5,4},{6,7},{7,6},{8,9},{9,8},{10,11... | collective-permute-start | bytes 24584 | tf_op jit(solution)/shard_map/ppermute | solution.py:290
  54.9 3.9 %collective-permute-start.8 = (bf16[1,16,128]{2,1,0:T(8,128)(2,1)S(1)}, bf16[1,16,128]{2,1,0:T(8,128)(2,1)S(1)}, u32[]{:S(2)}, u32[]{:S(2)}) collective-permute-start(bf16[1,16,128]{2,1,0:T(8,128)(2,1)S(1)} %get-tuple-element.60), channel_id=1, source_target_pairs={{4,8},{8,4},{12,16},{16,12},{20,24},{24,20},{28,0},{0,28},{5,9},{9... | collective-permute-start | bytes 12296 | tf_op jit(solution)/shard_map/ppermute | solution.py:290
  54.9 3.9 %collective-permute-start.11 = (bf16[1,16,128]{2,1,0:T(8,128)(2,1)S(1)}, bf16[1,16,128]{2,1,0:T(8,128)(2,1)S(1)}, u32[]{:S(2)}, u32[]{:S(2)}) collective-permute-start(bf16[1,16,128]{2,1,0:T(8,128)(2,1)S(1)} %get-tuple-element.63), channel_id=1, source_target_pairs={{0,4},{4,0},{8,12},{12,8},{16,20},{20,16},{24,28},{28,24},{1,5},{5... | collective-permute-start | bytes 12296 | tf_op jit(solution)/shard_map/ppermute | solution.py:290

commit v3 on v2

--- a/solution.py
+++ b/solution.py
@@ -7,13 +7,13 @@
 from jax.experimental.pallas import tpu as pltpu
 from jax.sharding import PartitionSpec as P
 
+
 SWEEPS = 3
 F32 = jnp.float32
 BF16 = jnp.bfloat16
 I32 = jnp.int32
 VMEM = pl.BlockSpec(memory_space=pltpu.VMEM)
 FAR = pl.BlockSpec(memory_space=pltpu.HBM)
-SMEM = pl.BlockSpec(memory_space=pltpu.SMEM)
 NT = (((1,), (1,)), ((), ()))
 NN = (((1,), (0,)), ((), ()))
 
@@ -38,30 +38,33 @@
     return [value[:, at : at + tile] for at in range(0, value.shape[1], tile)]
 
 
+def facing(groups):
+    return [
+        face ^ (lax.axis_index(axis) // apart % 2) for faces, axis, apart in groups for face in faces
+    ]
+
+
 def code_rows(parts):
     return -(-(2 + parts) // 16) * 16
 
 
 def first_kernel(
     groups,
-    place_ref,
     rhs_far,
     basis_far,
     inverse_far,
     weights_far,
     ids_far,
     faces_far,
-    chunk_far,
+    packed_ref,
     rhs_ref,
     basis_ref,
     weights_ref,
     ids_ref,
     masks_ref,
     inverse_ref,
-    packed_ref,
     faces_ref,
     in_sems,
-    out_sems,
 ):
     pairs = (
         (inverse_far, inverse_ref),
@@ -83,7 +86,7 @@
     copies[1].wait()
     ids = ids_ref[...]
     on_diagonal = lax.broadcasted_iota(I32, (held, total), 1) == (
-        lax.broadcasted_iota(I32, (held, total), 0) + place_ref[0] * held
+        lax.broadcasted_iota(I32, (held, total), 0) + lax.axis_index("sub") * held
     )
     inverse = inverse_ref[...]
     rounded = inverse.astype(BF16)
@@ -101,20 +104,11 @@
     copies[2].wait()
     copies[3].wait()
     packed_ref[head : head + rights] = matmul(rhs_ref[...].astype(BF16), basis_ref[...], NN).astype(BF16)
-    outs = [
-        pltpu.make_async_copy(packed_ref, chunk_far.at[i], out_sems.at[i])
-        for i in range(chunk_far.shape[0])
-    ]
-    for copy in outs:
-        copy.start()
     copies[4].wait()
     copies[5].wait()
-    flat = [(face, turn) for faces, turn in groups for face in faces]
     block = lax.broadcasted_iota(I32, masks_ref.shape[1:], 0)
-    for n, (face, turn) in enumerate(flat):
-        masks_ref[n] = (block == faces_ref[0, face ^ place_ref[turn]]).astype(F32)
-    for copy in outs:
-        copy.wait()
+    for n, face in enumerate(facing(groups)):
+        masks_ref[n] = (block == faces_ref[0, face]).astype(F32)
 
 
 def update(z, basis_ref, weights_ref, u, r, masks_ref, new_ref, out_refs):
@@ -132,7 +126,29 @@
             at += 1
 
 
-def opening_kernel(total, ids_ref, got_ref, basis_ref, weights_ref, r_ref, masks_ref, block_ref, new_ref, *out_refs):
+def opening_kernel(
+    total,
+    tiles_far,
+    match_far,
+    ids_ref,
+    got_ref,
+    basis_ref,
+    weights_ref,
+    r_ref,
+    masks_ref,
+    tiles_ref,
+    match_ref,
+    block_ref,
+    new_ref,
+    *refs,
+):
+    *out_refs, sems = refs
+    copies = [
+        pltpu.make_async_copy(tiles_far, tiles_ref, sems.at[0]),
+        pltpu.make_async_copy(match_far, match_ref, sems.at[1]),
+    ]
+    for copy in copies:
+        copy.start()
     peers = got_ref.shape[0]
     rights = r_ref.shape[0]
     count = ids_ref.shape[1]
@@ -163,6 +179,8 @@
         both = matmul(got_ref[i, head:body_at, :], piece, NT)
         z = z + both[:, :count] + both[:, count:]
     update(z, basis_ref, weights_ref, None, r_ref[...], masks_ref, new_ref, out_refs)
+    for copy in copies:
+        copy.wait()
 
 
 def correct_kernel(got_ref, block_ref, basis_ref, weights_ref, u_ref, r_ref, masks_ref, new_ref, *out_refs):
@@ -172,29 +190,26 @@
     update(z, basis_ref, weights_ref, u_ref[...], r_ref[...], masks_ref, new_ref, out_refs)
 
 
-def subtract_tile(t, list_ref, low_ref, tile_ref, rhs_ref, base_ref):
-    tile = tile_ref.shape[0]
-    product = matmul(low_ref[:, at_block(list_ref[1, t], tile)], tile_ref[...], NT)
-    if t * tile < base_ref.shape[1]:
-        cut = slice(t * tile, (t + 1) * tile)
-        base_ref[:, cut] = rhs_ref[:, cut] - product
-    else:
-        cut = at_block(list_ref[0, t], tile)
-        base_ref[:, cut] = base_ref[:, cut] - product
-
-
-def local_kernel(list_ref, u_ref, tiles_ref, rhs_ref, base_ref, low_ref):
-    low_ref[...] = u_ref[...].astype(BF16)
+def local_kernel(u_ref, rhs_ref, matrix_ref, base_ref, low_ref):
+    low = u_ref[...].astype(BF16)
+    low_ref[...] = low
+    base_ref[...] = rhs_ref[...] - matmul(low, matrix_ref[...], NT)
+
+
+def local_first_kernel(
+    groups, list_far, u_ref, rhs_ref, tiles_ref, match_ref, base_ref, low_ref, tables_ref, matrix_ref, list_ref, sem
+):
+    tile = tiles_ref.shape[1]
+    copy = pltpu.make_async_copy(list_far, list_ref, sem)
+    copy.start()
+    matrix_ref[...] = jnp.zeros_like(matrix_ref)
+    index = lax.broadcasted_iota(I32, tables_ref.shape[1:], 0)
+    for n, face in enumerate(facing(groups)):
+        tables_ref[n] = one_hot(index == match_ref[face])
+    copy.wait()
     for t in range(tiles_ref.shape[0]):
-        subtract_tile(t, list_ref, low_ref, tiles_ref.at[t], rhs_ref, base_ref)
-
-
-def local_first_kernel(groups, list_ref, place_ref, u_ref, tiles_ref, rhs_ref, match_ref, base_ref, low_ref, tables_ref):
-    flat = [(face, turn) for faces, turn in groups for face in faces]
-    index = lax.broadcasted_iota(I32, tables_ref.shape[1:], 0)
-    for n, (face, turn) in enumerate(flat):
-        tables_ref[n] = one_hot(index == match_ref[face ^ place_ref[turn]])
-    local_kernel(list_ref, u_ref, tiles_ref, rhs_ref, base_ref, low_ref)
+        matrix_ref[at_block(list_ref[0, t], tile), at_block(list_ref[1, t], tile)] = tiles_ref[t]
+    local_kernel(u_ref, rhs_ref, matrix_ref, base_ref, low_ref)
 
 
 def coupled(tables_ref, masks_ref, base_ref, in_refs):
@@ -226,12 +241,12 @@
     out_ref[...] = coupled(tables_ref, masks_ref, base_ref, in_refs).astype(BF16)
 
 
-def call(kernel, outs, args, scalars=0, far_args=0, far_outs=0, scratch=()):
+def call(kernel, outs, args, far_args=0, scratch=()):
     return pl.pallas_call(
         kernel,
         out_shape=outs,
-        in_specs=[SMEM] * scalars + [FAR] * far_args + [VMEM] * (len(args) - scalars - far_args),
-        out_specs=[FAR] * far_outs + [VMEM] * (len(outs) - far_outs),
+        in_specs=[FAR] * far_args + [VMEM] * (len(args) - far_args),
+        out_specs=[VMEM] * len(outs),
         scratch_shapes=list(scratch),
         compiler_params=pltpu.CompilerParams(vmem_limit_bytes=16 << 20),
     )(*args)
@@ -258,51 +273,43 @@
 ):
     order, rights = right_side.shape[2:]
     tile = tiles.shape[3]
-    listing = tile_list[0, 0].T
     count = coarse_map.shape[2]
     inverse_rows = coarse_inverse[0]
     held, total = inverse_rows.shape
     peers = lax.axis_size("sub")
     stride = max(lax.axis_size("reg") // 4, 1)
-    place = jnp.stack(
-        [lax.axis_index("sub"), lax.axis_index("sub") % 2]
-        + [lax.axis_index("reg") // far % 2 for far in sorted({1, stride})]
-    ).astype(I32)
     if stride == 1:
-        swaps = (((0, 2), "reg", 1, False, 2), ((1, 3), "reg", 1, True, 2))
+        swaps = (((0, 2), "reg", 1, False), ((1, 3), "reg", 1, True))
     else:
         swaps = (
-            ((0,), "reg", 1, False, 2),
-            ((2,), "reg", stride, False, 3),
-            ((1,), "reg", 1, True, 2),
-            ((3,), "reg", stride, True, 3),
+            ((0,), "reg", 1, False),
+            ((2,), "reg", stride, False),
+            ((1,), "reg", 1, True),
+            ((3,), "reg", stride, True),
         )
-    swaps = ((((4,), "sub", 1, False, 1),) + swaps + (((5,), "sub", 1, True, 1),))
-    groups = tuple((faces, turn) for faces, _, _, _, turn in swaps)
-
-    def swap(shard, axis, far, ahead):
+    swaps = (((4,), "sub", 1, False),) + swaps + (((5,), "sub", 1, True),)
+    groups = tuple(how[:3] for how in swaps)
+
+    def swap(shard, axis, apart, ahead):
         n = lax.axis_size(axis)
-        assert n // far % 2 == 0
+        assert n // apart % 2 == 0
         pairs = []
         for i in range(n):
-            if (i // far % 2 == 0) == ahead:
-                pairs += [(i, (i + far) % n), ((i + far) % n, i)]
+            if (i // apart % 2 == 0) == ahead:
+                pairs += [(i, (i + apart) % n), ((i + apart) % n, i)]
         return lax.ppermute(shard, axis, pairs)
 
     near_out, far_out = pltpu.VMEM, jax.ShapeDtypeStruct
     field = near_out((rights, order), F32)
-    face_outs = [far_out((len(faces), rights, tile), BF16) for faces, _ in groups]
-    face_count = sum(len(faces) for faces, _ in groups)
+    face_outs = [far_out((len(faces), rights, tile), BF16) for faces, _, _ in groups]
+    face_count = sum(len(faces) for faces, _, _ in groups)
     parts = total // count
     rows = code_rows(parts) + rights + held * parts
 
-    def spread(chunk):
-        return near(lax.all_to_all(chunk, "sub", split_axis=0, concat_axis=0, tiled=True))
-
-    chunk, rhs, basis, scaling, ids, masks = call(
+    packed, rhs, basis, scaling, ids, masks = call(
         functools.partial(first_kernel, groups),
         [
-            far_out((peers, rows, count), BF16),
+            far_out((rows, count), BF16),
             field,
             near_out((order, count), BF16),
             near_out((1, order), F32),
@@ -310,7 +317,6 @@
             near_out((face_count, -(-(order // tile) // 8) * 8, tile), F32),
         ],
         [
-            place,
             far(right_side[0, 0].T),
             far(coarse_basis[0, 0]),
             far(inverse_rows),
@@ -318,42 +324,58 @@
             far(coarse_map[0]),
             far(face_map[0]),
         ],
-        scalars=1,
         far_args=6,
-        far_outs=1,
         scratch=[
             pltpu.VMEM((held, total), F32),
-            pltpu.VMEM((rows, count), BF16),
             pltpu.SMEM(face_map.shape[1:], I32),
             pltpu.SemaphoreType.DMA((6,)),
-            pltpu.SemaphoreType.DMA((peers,)),
         ],
     )
-    tile_block = tiles[0, 0]
     residual = rhs
     for sweep in range(SWEEPS):
-        got = spread(chunk)
         if sweep == 0:
-            block, u, *faces = call(
+            got = near(lax.all_gather(packed, "sub", axis=0))
+            tile_block, matched, block, u, *faces = call(
                 functools.partial(opening_kernel, total),
-                [near_out((peers, 2 * count, count), BF16), field, *face_outs],
-                [ids, got, basis, scaling, residual, masks],
+                [
+                    near_out(tiles.shape[2:], BF16),
+                    near_out((matching.shape[2], 1, tile), I32),
+                    near_out((peers, 2 * count, count), BF16),
+                    field,
+                    *face_outs,
+                ],
+                [
+                    far(tiles[0, 0]),
+                    far(matching[0].reshape(-1, 1, tile)),
+                    ids,
+                    got,
+                    basis,
+                    scaling,
+                    residual,
+                    masks,
+                ],
+                far_args=2,
+                scratch=[pltpu.SemaphoreType.DMA((2,))],
             )
         else:
+            got = near(lax.all_to_all(chunk, "sub", split_axis=0, concat_axis=0, tiled=True))
             u, *faces = call(
                 correct_kernel, [field, *face_outs], [got, block, basis, scaling, u, residual, masks]
             )
-        arrived = [near(swap(face, *how[1:4])) for face, how in zip(faces, swaps, strict=True)]
+        arrived = []
+        for face, how in zip(faces, swaps, strict=True):
+            arrived.append(near(swap(face, *how[1:4])))
         low_out = (near_out if sweep + 1 < SWEEPS else far_out)((rights, order), BF16)
         if sweep == 0:
-            base, low, tables = call(
+            base, low, tables, matrix = call(
                 functools.partial(local_first_kernel, groups),
-                [field, low_out, near_out((face_count, tile, tile), BF16)],
-                [listing, place, u, tile_block, rhs, matching[0].reshape(-1, 1, tile)],
-                scalars=2,
+                [field, low_out, near_out((face_count, tile, tile), BF16), near_out((order, order), BF16)],
+                [far(tile_list[0, 0].T), u, rhs, tile_block, matched],
+                far_args=1,
+                scratch=[pltpu.SMEM(tile_list.shape[:1:-1], I32), pltpu.SemaphoreType.DMA],
             )
         else:
-            base, low = call(local_kernel, [field, low_out], [listing, u, tile_block, rhs], scalars=1)
+            base, low = call(local_kernel, [field, low_out], [u, rhs, matrix])
         if sweep + 1 < SWEEPS:
             residual, chunk = call(
                 residual_kernel,

time: 59.8 us -> 53.8 us (0.90)
  Pallas kernels: 15.2 us -> 10.3 us
  blocking collectives: 30.5 us -> 26.1 us
  waiting for transfers between devices: 2.21 us -> 4.71 us
  starting transfers between devices: 10.8 us -> 11.7 us
    all_to_all x3 -> x2, blocking collectives: 30.5 us -> 14.6 us  [body(): lax.all_to_all(chunk, 'sub', split_axis=0, concat_axis=0, tiled=True)]
    all_gather x0 -> x1, blocking collectives: none -> 11.5 us  [body(): got = near(lax.all_gather(packed, 'sub', axis=0))]
    pallas_call x10, Pallas kernels: 15.2 us -> 10.3 us  [call(): pl.pallas_call(kernel, out_shape=outs, in_specs=[FAR] * far_args + [VMEM]...]
    ppermute x12, waiting for transfers between devices: 2.21 us -> 4.71 us  [swap(): return lax.ppermute(shard, axis, pairs)]
    ppermute x12, starting transfers between devices: 10.8 us -> 11.7 us  [swap(): return lax.ppermute(shard, axis, pairs)]
  transfers between devices with their start and end apart: 12 -> 12, of which waited for: 3 -> 3; matrix products, arithmetic and copies ran while one was open for 0% -> 0% of each run, Pallas kernels for 13% -> 8%
where the time goes in v3:
time: 53.8 us; the launch traced here: 53.6 us
  blocking collectives  26.1 us (49%)
  starting transfers between devices  11.7 us (22%)
  Pallas kernels  10.3 us (19%)
  waiting for transfers between devices  4.71 us (9%)
  between operations  0.71 us (1%)
    all_to_all x2, blocking collectives, body(): lax.all_to_all(chunk, 'sub', split_axis=0, concat_axis=0, tiled=True)  14.6 us
    ppermute x12, starting transfers between devices, swap(): return lax.ppermute(shard, axis, pairs)  11.7 us
    all_gather x1, blocking collectives, body(): got = near(lax.all_gather(packed, 'sub', axis=0))  11.5 us
    pallas_call x10, Pallas kernels, call(): pl.pallas_call(kernel, out_shape=outs, in_specs=[FAR] * far_args + [VMEM]...  10.3 us
    ppermute x12, waiting for transfers between devices, swap(): return lax.ppermute(shard, axis, pairs)  4.71 us
  transfers between devices with their start and end apart: 12, of which 3 were waited for; matrix products, arithmetic and copies ran while one was open for 0% of the time, Pallas kernels for 8%

profile of v3, /device:TPU:0, one launch (start us, length us, event | category | flops | bytes accessed | tf_op | source)
XLA Modules:
  0.0 53.6 jit_solution(11624680715787094751)
XLA Ops:
  0.6 1.4 %shard_map.104 = (bf16[288,128]{1,0:T(8,128)(2,1)S(1)}, f32[16,1280]{1,0:T(8,128)S(1)}, bf16[1280,128]{1,0:T(8,128)(2,1)S(1)}, f32[1,1280]{1,0:T(1,128)S(1)}, s3...) custom-call(f32[16,1280]{1,0:T(8,128)} %bitcast.24, bf16[1280,128]{1,0:T(8,128)(2,1)} %bitcast.22, f32[64,512]{1,0:T(8,128)} %bitcast.23, ...), custom_call_target="tpu_custom_call" | custom-call | tf_op jit(solution)/shard_map/pallas_call | solution.py:245
  2.0 11.5 %all-gather = bf16[2304,128]{1,0:T(8,128)(2,1)S(1)} all-gather(bf16[288,128]{1,0:T(8,128)(2,1)S(1)} %get-tuple-element.37), channel_id=2, replica_groups=mesh['sub'=8,'reg'=4] {'sub'}, dimensions={0}, use_global_device_ids=true | all-gather | bytes 663552 | tf_op jit(solution)/shard_map/all_gather | solution.py:337
  13.5 2.3 %shard_map.105 = (bf16[80,128,128]{2,1,0:T(8,128)(2,1)S(1)}, s32[6,1,128]{2,1,0:T(1,128)S(1)}, bf16[8,256,128]{2,1,0:T(8,128)(2,1)S(1)}, f32[16,1280]{1,0:T(8,12...) custom-call(bf16[80,128,128]{2,1,0:T(8,128)(2,1)} %bitcast.21, ...), custom_call_target="tpu_custom_call" | custom-call | tf_op jit(solution)/shard_map/pallas_call | solution.py:245
  15.7 3.7 %collective-permute-start.1 = (bf16[2,16,128]{2,1,0:T(8,128)(2,1)S(1)}, bf16[2,16,128]{2,1,0:T(8,128)(2,1)S(1)}, u32[]{:S(2)}, u32[]{:S(2)}) collective-permute-start(bf16[2,16,128]{2,1,0:T(8,128)(2,1)S(1)} %get-tuple-element.48), channel_id=1, source_target_pairs={{1,2},{2,1},{3,0},{0,3},{5,6},{6,5},{7,4},{4,7},{9,10},{10,9},{11,... | collective-permute-start | bytes 24584 | tf_op jit(solution)/shard_map/ppermute | solution.py:300
  19.4 1.1 %collective-permute-start = (bf16[1,16,128]{2,1,0:T(8,128)(2,1)S(1)}, bf16[1,16,128]{2,1,0:T(8,128)(2,1)S(1)}, u32[]{:S(2)}, u32[]{:S(2)}) collective-permute-start(bf16[1,16,128]{2,1,0:T(8,128)(2,1)S(1)} %get-tuple-element.47), channel_id=1, source_target_pairs={{4,8},{8,4},{12,16},{16,12},{20,24},{24,20},{28,0},{0,28},{5,9},{9... | collective-permute-start | bytes 12296 | tf_op jit(solution)/shard_map/ppermute | solution.py:300
  20.5 0.5 collective-permute-start.3
  21.0 2.2 %shard_map.106 = (f32[16,1280]{1,0:T(8,128)S(1)}, bf16[16,1280]{1,0:T(8,128)(2,1)}, bf16[6,128,128]{2,1,0:T(8,128)(2,1)S(1)}, bf16[1280,1280]{1,0:T(8,128)(2,1)S(1)}) custom-call(s32[2,80]{1,0:T(2,128)} %bitcast.28, f32[16,1280]{1,0:T(8,128)S(1)} %get-tuple-element.42.u_ref, f32[16,1280]{1,0:T(8,128)S(1)} %get-tuple-element.40.r_ref.rhs_ref, ...), custom_call_target="tpu_custom_call" | custom-call | tf_op jit(solution)/shard_map/pallas_call | solution.py:245
  23.2 0.1 collective-permute-done.refs_0_
  23.3 0.3 shard_map.107
  23.7 7.4 %all_to_all.10.got_ref = bf16[8,16,128]{2,1,0:T(8,128)(2,1)S(1)} all-to-all(bf16[8,16,128]{2,1,0:T(8,128)(2,1)S(1)} %get-tuple-element.51), channel_id=1, replica_groups=mesh['sub'=8,'reg'=4] {'sub'}, dimensions={0} | all-to-all | bytes 65536 | tf_op jit(solution)/shard_map/all_to_all | solution.py:361
  31.1 0.6 %shard_map.108 = (f32[16,1280]{1,0:T(8,128)S(1)}, bf16[1,16,128]{2,1,0:T(8,128)(2,1)S(1)}, bf16[2,16,128]{2,1,0:T(8,128)(2,1)S(1)}, bf16[2,16,128]{2,1,0:T(8,128)(2,1)S(1)}, bf16[1,16,128]{2,1,0:T(8,128)(2,1)S(1)}) custom-call(bf16[8,16,128]{2,1,0:T(8,128)(2,1)S(1)} %all_to_all.10.got_ref, bf16[8,256,128]{2,1,0:T(8,128)(2,1)S(1)} %get-tuple-element.52.block_ref, ...), custom_call_target="tpu_custom_call" | custom-call | tf_op jit(solution)/shard_map/pallas_call | solution.py:245
  31.7 1.6 %collective-permute-start.5 = (bf16[2,16,128]{2,1,0:T(8,128)(2,1)S(1)}, bf16[2,16,128]{2,1,0:T(8,128)(2,1)S(1)}, u32[]{:S(2)}, u32[]{:S(2)}) collective-permute-start(bf16[2,16,128]{2,1,0:T(8,128)(2,1)S(1)} %get-tuple-element.58), channel_id=1, source_target_pairs={{1,2},{2,1},{3,0},{0,3},{5,6},{6,5},{7,4},{4,7},{9,10},{10,9},{11,... | collective-permute-start | bytes 24584 | tf_op jit(solution)/shard_map/ppermute | solution.py:300
  33.2 0.6 %collective-permute-start.6 = (bf16[2,16,128]{2,1,0:T(8,128)(2,1)S(1)}, bf16[2,16,128]{2,1,0:T(8,128)(2,1)S(1)}, u32[]{:S(2)}, u32[]{:S(2)}) collective-permute-start(bf16[2,16,128]{2,1,0:T(8,128)(2,1)S(1)} %get-tuple-element.59), channel_id=1, source_target_pairs={{0,1},{1,0},{2,3},{3,2},{4,5},{5,4},{6,7},{7,6},{8,9},{9,8},{10,11... | collective-permute-start | bytes 24584 | tf_op jit(solution)/shard_map/ppermute | solution.py:300
  33.8 0.7 %collective-permute-start.7 = (bf16[1,16,128]{2,1,0:T(8,128)(2,1)S(1)}, bf16[1,16,128]{2,1,0:T(8,128)(2,1)S(1)}, u32[]{:S(2)}, u32[]{:S(2)}) collective-permute-start(bf16[1,16,128]{2,1,0:T(8,128)(2,1)S(1)} %get-tuple-element.60), channel_id=1, source_target_pairs={{0,4},{4,0},{8,12},{12,8},{16,20},{20,16},{24,28},{28,24},{1,5},{5... | collective-permute-start | bytes 12296 | tf_op jit(solution)/shard_map/ppermute | solution.py:300
  34.5 1.0 %shard_map.109 = (f32[16,1280]{1,0:T(8,128)S(1)}, bf16[16,1280]{1,0:T(8,128)(2,1)}) custom-call(f32[16,1280]{1,0:T(8,128)S(1)} %get-tuple-element.54.u_ref, f32[16,1280]{1,0:T(8,128)S(1)} %get-tuple-element.40.r_ref.rhs_ref, bf16[1280,1280]{1,0:T(8,128)(2,1)S(1)} %get-tuple-element.55.matrix_ref), custom_call_target="tpu_custom_call" | custom-call | tf_op jit(solution)/shard_map/pallas_call | solution.py:245
  35.5 2.3 %collective-permute-done.4.refs_0_ = bf16[1,16,128]{2,1,0:T(8,128)(2,1)S(1)} collective-permute-done((bf16[1,16,128]{2,1,0:T(8,128)(2,1)S(1)}, bf16[1,16,128]{2,1,0:T(8,128)(2,1)S(1)}, u32[]{:S(2)}, u32[]{:S(2)}) %collective-permute-start.4) | collective-permute-done | bytes 4128 | tf_op jit(solution)/shard_map/ppermute | solution.py:300
  37.8 0.3 shard_map.110
  38.1 7.2 %all_to_all.11.got_ref = bf16[8,16,128]{2,1,0:T(8,128)(2,1)S(1)} all-to-all(bf16[8,16,128]{2,1,0:T(8,128)(2,1)S(1)} %get-tuple-element.61), channel_id=1, replica_groups=mesh['sub'=8,'reg'=4] {'sub'}, dimensions={0} | all-to-all | bytes 65536 | tf_op jit(solution)/shard_map/all_to_all | solution.py:361
  45.3 0.6 %shard_map.111 = (f32[16,1280]{1,0:T(8,128)S(1)}, bf16[1,16,128]{2,1,0:T(8,128)(2,1)S(1)}, bf16[2,16,128]{2,1,0:T(8,128)(2,1)S(1)}, bf16[2,16,128]{2,1,0:T(8,128)(2,1)S(1)}, bf16[1,16,128]{2,1,0:T(8,128)(2,1)S(1)}) custom-call(bf16[8,16,128]{2,1,0:T(8,128)(2,1)S(1)} %all_to_all.11.got_ref, bf16[8,256,128]{2,1,0:T(8,128)(2,1)S(1)} %get-tuple-element.52.block_ref, ...), custom_call_target="tpu_custom_call" | custom-call | tf_op jit(solution)/shard_map/pallas_call | solution.py:245
  45.9 2.9 %collective-permute-start.9 = (bf16[2,16,128]{2,1,0:T(8,128)(2,1)S(1)}, bf16[2,16,128]{2,1,0:T(8,128)(2,1)S(1)}, u32[]{:S(2)}, u32[]{:S(2)}) collective-permute-start(bf16[2,16,128]{2,1,0:T(8,128)(2,1)S(1)} %get-tuple-element.67), channel_id=1, source_target_pairs={{1,2},{2,1},{3,0},{0,3},{5,6},{6,5},{7,4},{4,7},{9,10},{10,9},{11,... | collective-permute-start | bytes 24584 | tf_op jit(solution)/shard_map/ppermute | solution.py:300
  48.8 0.7 %collective-permute-start.11 = (bf16[1,16,128]{2,1,0:T(8,128)(2,1)S(1)}, bf16[1,16,128]{2,1,0:T(8,128)(2,1)S(1)}, u32[]{:S(2)}, u32[]{:S(2)}) collective-permute-start(bf16[1,16,128]{2,1,0:T(8,128)(2,1)S(1)} %get-tuple-element.69), channel_id=1, source_target_pairs={{0,4},{4,0},{8,12},{12,8},{16,20},{20,16},{24,28},{28,24},{1,5},{5... | collective-permute-start | bytes 12296 | tf_op jit(solution)/shard_map/ppermute | solution.py:300
  49.5 1.0 %shard_map.112 = (f32[16,1280]{1,0:T(8,128)S(1)}, bf16[16,1280]{1,0:T(8,128)(2,1)}) custom-call(f32[16,1280]{1,0:T(8,128)S(1)} %get-tuple-element.63.u_ref, f32[16,1280]{1,0:T(8,128)S(1)} %get-tuple-element.40.r_ref.rhs_ref, bf16[1280,1280]{1,0:T(8,128)(2,1)S(1)} %get-tuple-element.55.matrix_ref), custom_call_target="tpu_custom_call" | custom-call | tf_op jit(solution)/shard_map/pallas_call | solution.py:245
  50.5 2.3 %collective-permute-done.8.refs_0_ = bf16[1,16,128]{2,1,0:T(8,128)(2,1)S(1)} collective-permute-done((bf16[1,16,128]{2,1,0:T(8,128)(2,1)S(1)}, bf16[1,16,128]{2,1,0:T(8,128)(2,1)S(1)}, u32[]{:S(2)}, u32[]{:S(2)}) %collective-permute-start.8) | collective-permute-done | bytes 4128 | tf_op jit(solution)/shard_map/ppermute | solution.py:300
  52.8 0.8 %shard_map.113 = bf16[16,1280]{1,0:T(8,128)(2,1)} custom-call(bf16[6,128,128]{2,1,0:T(8,128)(2,1)S(1)} %get-tuple-element.45.tables_ref, f32[6,16,128]{2,1,0:T(8,128)S(1)} %get-tuple-element.41.masks_ref, f32[16,1280]{1,0:T(8,128)S(1)} %get-tuple-element.65.base_ref, bf16[1,16,128]{2,1,0:T(8,128)(2,1)S(1)} %collective-permute-done.8.refs_0_, ...), custom_call_target="tpu_custom_call" | custom-call | tf_op jit(solution)/shard_map/pallas_call | solution.py:245
  (13 shorter events, 0.0 us)
Async XLA Ops:
  15.7 7.6 %collective-permute-start.1 = (bf16[2,16,128]{2,1,0:T(8,128)(2,1)S(1)}, bf16[2,16,128]{2,1,0:T(8,128)(2,1)S(1)}, u32[]{:S(2)}, u32[]{:S(2)}) collective-permute-start(bf16[2,16,128]{2,1,0:T(8,128)(2,1)S(1)} %get-tuple-element.48), channel_id=1, source_target_pairs={{1,2},{2,1},{3,0},{0,3},{5,6},{6,5},{7,4},{4,7},{9,10},{10,9},{11,... | collective-permute-start | bytes 24584 | tf_op jit(solution)/shard_map/ppermute | solution.py:300
  19.4 3.9 %collective-permute-start.2 = (bf16[2,16,128]{2,1,0:T(8,128)(2,1)S(1)}, bf16[2,16,128]{2,1,0:T(8,128)(2,1)S(1)}, u32[]{:S(2)}, u32[]{:S(2)}) collective-permute-start(bf16[2,16,128]{2,1,0:T(8,128)(2,1)S(1)} %get-tuple-element.49), channel_id=1, source_target_pairs={{0,1},{1,0},{2,3},{3,2},{4,5},{5,4},{6,7},{7,6},{8,9},{9,8},{10,11... | collective-permute-start | bytes 24584 | tf_op jit(solution)/shard_map/ppermute | solution.py:300
  19.4 3.9 %collective-permute-start = (bf16[1,16,128]{2,1,0:T(8,128)(2,1)S(1)}, bf16[1,16,128]{2,1,0:T(8,128)(2,1)S(1)}, u32[]{:S(2)}, u32[]{:S(2)}) collective-permute-start(bf16[1,16,128]{2,1,0:T(8,128)(2,1)S(1)} %get-tuple-element.47), channel_id=1, source_target_pairs={{4,8},{8,4},{12,16},{16,12},{20,24},{24,20},{28,0},{0,28},{5,9},{9... | collective-permute-start | bytes 12296 | tf_op jit(solution)/shard_map/ppermute | solution.py:300
  20.5 2.8 %collective-permute-start.3 = (bf16[1,16,128]{2,1,0:T(8,128)(2,1)S(1)}, bf16[1,16,128]{2,1,0:T(8,128)(2,1)S(1)}, u32[]{:S(2)}, u32[]{:S(2)}) collective-permute-start(bf16[1,16,128]{2,1,0:T(8,128)(2,1)S(1)} %get-tuple-element.50), channel_id=1, source_target_pairs={{0,4},{4,0},{8,12},{12,8},{16,20},{20,16},{24,28},{28,24},{1,5},{5... | collective-permute-start | bytes 12296 | tf_op jit(solution)/shard_map/ppermute | solution.py:300
  31.7 6.1 %collective-permute-start.5 = (bf16[2,16,128]{2,1,0:T(8,128)(2,1)S(1)}, bf16[2,16,128]{2,1,0:T(8,128)(2,1)S(1)}, u32[]{:S(2)}, u32[]{:S(2)}) collective-permute-start(bf16[2,16,128]{2,1,0:T(8,128)(2,1)S(1)} %get-tuple-element.58), channel_id=1, source_target_pairs={{1,2},{2,1},{3,0},{0,3},{5,6},{6,5},{7,4},{4,7},{9,10},{10,9},{11,... | collective-permute-start | bytes 24584 | tf_op jit(solution)/shard_map/ppermute | solution.py:300
  33.2 4.5 %collective-permute-start.6 = (bf16[2,16,128]{2,1,0:T(8,128)(2,1)S(1)}, bf16[2,16,128]{2,1,0:T(8,128)(2,1)S(1)}, u32[]{:S(2)}, u32[]{:S(2)}) collective-permute-start(bf16[2,16,128]{2,1,0:T(8,128)(2,1)S(1)} %get-tuple-element.59), channel_id=1, source_target_pairs={{0,1},{1,0},{2,3},{3,2},{4,5},{5,4},{6,7},{7,6},{8,9},{9,8},{10,11... | collective-permute-start | bytes 24584 | tf_op jit(solution)/shard_map/ppermute | solution.py:300
  33.8 3.9 %collective-permute-start.4 = (bf16[1,16,128]{2,1,0:T(8,128)(2,1)S(1)}, bf16[1,16,128]{2,1,0:T(8,128)(2,1)S(1)}, u32[]{:S(2)}, u32[]{:S(2)}) collective-permute-start(bf16[1,16,128]{2,1,0:T(8,128)(2,1)S(1)} %get-tuple-element.57), channel_id=1, source_target_pairs={{4,8},{8,4},{12,16},{16,12},{20,24},{24,20},{28,0},{0,28},{5,9},{9... | collective-permute-start | bytes 12296 | tf_op jit(solution)/shard_map/ppermute | solution.py:300
  33.8 3.9 %collective-permute-start.7 = (bf16[1,16,128]{2,1,0:T(8,128)(2,1)S(1)}, bf16[1,16,128]{2,1,0:T(8,128)(2,1)S(1)}, u32[]{:S(2)}, u32[]{:S(2)}) collective-permute-start(bf16[1,16,128]{2,1,0:T(8,128)(2,1)S(1)} %get-tuple-element.60), channel_id=1, source_target_pairs={{0,4},{4,0},{8,12},{12,8},{16,20},{20,16},{24,28},{28,24},{1,5},{5... | collective-permute-start | bytes 12296 | tf_op jit(solution)/shard_map/ppermute | solution.py:300
  45.9 6.9 %collective-permute-start.9 = (bf16[2,16,128]{2,1,0:T(8,128)(2,1)S(1)}, bf16[2,16,128]{2,1,0:T(8,128)(2,1)S(1)}, u32[]{:S(2)}, u32[]{:S(2)}) collective-permute-start(bf16[2,16,128]{2,1,0:T(8,128)(2,1)S(1)} %get-tuple-element.67), channel_id=1, source_target_pairs={{1,2},{2,1},{3,0},{0,3},{5,6},{6,5},{7,4},{4,7},{9,10},{10,9},{11,... | collective-permute-start | bytes 24584 | tf_op jit(solution)/shard_map/ppermute | solution.py:300
  48.8 3.9 %collective-permute-start.10 = (bf16[2,16,128]{2,1,0:T(8,128)(2,1)S(1)}, bf16[2,16,128]{2,1,0:T(8,128)(2,1)S(1)}, u32[]{:S(2)}, u32[]{:S(2)}) collective-permute-start(bf16[2,16,128]{2,1,0:T(8,128)(2,1)S(1)} %get-tuple-element.68), channel_id=1, source_target_pairs={{0,1},{1,0},{2,3},{3,2},{4,5},{5,4},{6,7},{7,6},{8,9},{9,8},{10,11... | collective-permute-start | bytes 24584 | tf_op jit(solution)/shard_map/ppermute | solution.py:300
  48.8 3.9 %collective-permute-start.8 = (bf16[1,16,128]{2,1,0:T(8,128)(2,1)S(1)}, bf16[1,16,128]{2,1,0:T(8,128)(2,1)S(1)}, u32[]{:S(2)}, u32[]{:S(2)}) collective-permute-start(bf16[1,16,128]{2,1,0:T(8,128)(2,1)S(1)} %get-tuple-element.66), channel_id=1, source_target_pairs={{4,8},{8,4},{12,16},{16,12},{20,24},{24,20},{28,0},{0,28},{5,9},{9... | collective-permute-start | bytes 12296 | tf_op jit(solution)/shard_map/ppermute | solution.py:300
  48.8 3.9 %collective-permute-start.11 = (bf16[1,16,128]{2,1,0:T(8,128)(2,1)S(1)}, bf16[1,16,128]{2,1,0:T(8,128)(2,1)S(1)}, u32[]{:S(2)}, u32[]{:S(2)}) collective-permute-start(bf16[1,16,128]{2,1,0:T(8,128)(2,1)S(1)} %get-tuple-element.69), channel_id=1, source_target_pairs={{0,4},{4,0},{8,12},{12,8},{16,20},{20,16},{24,28},{28,24},{1,5},{5... | collective-permute-start | bytes 12296 | tf_op jit(solution)/shard_map/ppermute | solution.py:300

commit v4 on v3

--- a/solution.py
+++ b/solution.py
@@ -9,6 +9,7 @@
 
 
 SWEEPS = 3
+FETCH = 10
 F32 = jnp.float32
 BF16 = jnp.bfloat16
 I32 = jnp.int32
@@ -42,6 +43,12 @@
     return [
         face ^ (lax.axis_index(axis) // apart % 2) for faces, axis, apart in groups for face in faces
     ]
+
+
+def inverse_columns(got_ref, at, parts, q):
+    peers, rows, count = got_ref.shape
+    held = (rows - at) // parts
+    return got_ref[:, at + q * held : at + (q + 1) * held, :].reshape(peers * held, count)
 
 
 def code_rows(parts):
@@ -136,56 +143,55 @@
     weights_ref,
     r_ref,
     masks_ref,
+    matrix_ref,
     tiles_ref,
     match_ref,
-    block_ref,
+    where_ref,
+    own_ref,
     new_ref,
     *refs,
 ):
     *out_refs, sems = refs
     copies = [
-        pltpu.make_async_copy(tiles_far, tiles_ref, sems.at[0]),
-        pltpu.make_async_copy(match_far, match_ref, sems.at[1]),
+        pltpu.make_async_copy(match_far, match_ref, sems.at[0]),
+        pltpu.make_async_copy(tiles_far.at[pl.ds(0, tiles_ref.shape[0])], tiles_ref, sems.at[1]),
     ]
     for copy in copies:
         copy.start()
+    matrix_ref[...] = jnp.zeros_like(matrix_ref)
     peers = got_ref.shape[0]
     rights = r_ref.shape[0]
     count = ids_ref.shape[1]
     parts = total // count
     head = code_rows(parts)
-    body_at = head + rights
-    held = (got_ref.shape[1] - body_at) // parts
     codes = [got_ref[i, :head, :].astype(F32) for i in range(peers)]
-    dropped = sum(codes)
+    index = lax.broadcasted_iota(I32, (total, count), 0).astype(F32)
+    for i in range(peers):
+        ids = codes[i][0:1] * 128.0 + codes[i][1:2]
+        where_ref[:, i * count : (i + 1) * count] = one_hot(index == ids)
     column = jnp.broadcast_to(ids_ref[...].astype(F32), (count, count)).T
     lane = lax.broadcasted_iota(I32, (count, count), 1).astype(F32)
-    own = [column == lane + float(q * count) for q in range(parts)]
-    own_low = jnp.concatenate([one_hot(hot) for hot in own], axis=1)
-    own_rows, own_dropped = [], []
     for q in range(parts):
-        piece = got_ref[:, body_at + q * held : body_at + (q + 1) * held, :].reshape(peers * held, count)
-        own_rows.append(matmul(own_low, piece, NN).astype(BF16))
-        own_dropped.append(jnp.where(own[q], dropped[2 + q : 3 + q], 0.0).astype(BF16))
-    own_rows = jnp.concatenate(
-        [jnp.concatenate(own_rows, axis=1), jnp.concatenate(own_dropped, axis=1)], axis=0
-    )
-    index = lax.broadcasted_iota(I32, (total, count), 0).astype(F32)
-    z = jnp.zeros((rights, count), F32)
-    for i in range(peers):
-        ids = codes[i][0:1] * 128.0 + codes[i][1:2]
-        piece = matmul(own_rows, one_hot(index == ids), NN).astype(BF16)
-        block_ref[i] = piece
-        both = matmul(got_ref[i, head:body_at, :], piece, NT)
-        z = z + both[:, :count] + both[:, count:]
-    update(z, basis_ref, weights_ref, None, r_ref[...], masks_ref, new_ref, out_refs)
+        own_ref[:, q * count : (q + 1) * count] = one_hot(column == lane + float(q * count))
+    coarse = jnp.concatenate([got_ref[i, head : head + rights, :] for i in range(peers)], axis=1)
+    assembled = matmul(coarse, where_ref[...], NT)
+    high = assembled.astype(BF16)
+    both = jnp.concatenate([high, (assembled - high.astype(F32)).astype(BF16)], axis=0)
+    dropped = sum(codes)
+    z = []
+    for q, part in enumerate(blocks_of(assembled, count)):
+        product = matmul(both, inverse_columns(got_ref, head + rights, parts, q), NN)
+        z.append(product[:rights] + product[rights:] + dropped[2 + q : 3 + q] * part)
+    z = jnp.concatenate(z, axis=1).astype(BF16)
+    z_own = matmul(z, own_ref[...], NT)
+    update(z_own, basis_ref, weights_ref, None, r_ref[...], masks_ref, new_ref, out_refs)
     for copy in copies:
         copy.wait()
 
 
 def correct_kernel(got_ref, block_ref, basis_ref, weights_ref, u_ref, r_ref, masks_ref, new_ref, *out_refs):
     count = got_ref.shape[2]
-    both = matmul(lanes(got_ref), lanes(block_ref), NT)
+    both = matmul(lanes(got_ref), block_ref[...], NT)
     z = both[:, :count] + both[:, count:]
     update(z, basis_ref, weights_ref, u_ref[...], r_ref[...], masks_ref, new_ref, out_refs)
 
@@ -197,18 +203,59 @@
 
 
 def local_first_kernel(
-    groups, list_far, u_ref, rhs_ref, tiles_ref, match_ref, base_ref, low_ref, tables_ref, matrix_ref, list_ref, sem
+    groups,
+    total,
+    tiles_far,
+    list_far,
+    u_ref,
+    rhs_ref,
+    empty_ref,
+    tiles_ref,
+    match_ref,
+    got_ref,
+    where_ref,
+    own_ref,
+    base_ref,
+    low_ref,
+    tables_ref,
+    block_ref,
+    matrix_ref,
+    list_ref,
+    rest_ref,
+    sems,
 ):
-    tile = tiles_ref.shape[1]
-    copy = pltpu.make_async_copy(list_far, list_ref, sem)
-    copy.start()
-    matrix_ref[...] = jnp.zeros_like(matrix_ref)
+    first, rest = tiles_ref.shape[0], rest_ref.shape[0]
+    copies = [
+        pltpu.make_async_copy(list_far, list_ref, sems.at[0]),
+        pltpu.make_async_copy(tiles_far.at[pl.ds(first, rest)], rest_ref, sems.at[1]),
+    ]
+    for copy in copies:
+        copy.start()
     index = lax.broadcasted_iota(I32, tables_ref.shape[1:], 0)
     for n, face in enumerate(facing(groups)):
         tables_ref[n] = one_hot(index == match_ref[face])
-    copy.wait()
-    for t in range(tiles_ref.shape[0]):
+    peers, _, count = got_ref.shape
+    parts = total // count
+    head = code_rows(parts)
+    own = own_ref[...]
+    dropped = sum(got_ref[i, :head, :].astype(F32) for i in range(peers))
+    own_rows, own_dropped = [], []
+    for q in range(parts):
+        piece = inverse_columns(got_ref, head + rhs_ref.shape[0], parts, q)
+        own_rows.append(matmul(own, piece, NN).astype(BF16))
+        own_dropped.append(own[:, q * count : (q + 1) * count] * dropped[2 + q : 3 + q].astype(BF16))
+    rows = jnp.concatenate(
+        [jnp.concatenate(own_rows, axis=1), jnp.concatenate(own_dropped, axis=1)], axis=0
+    )
+    block_ref[...] = matmul(rows, where_ref[...], NN).astype(BF16)
+    tile = tiles_ref.shape[1]
+    copies[0].wait()
+    for t in range(first):
         matrix_ref[at_block(list_ref[0, t], tile), at_block(list_ref[1, t], tile)] = tiles_ref[t]
+    copies[1].wait()
+    for t in range(rest):
+        at = at_block(list_ref[0, first + t], tile), at_block(list_ref[1, first + t], tile)
+        matrix_ref[at] = rest_ref[t]
     local_kernel(u_ref, rhs_ref, matrix_ref, base_ref, low_ref)
 
 
@@ -241,13 +288,14 @@
     out_ref[...] = coupled(tables_ref, masks_ref, base_ref, in_refs).astype(BF16)
 
 
-def call(kernel, outs, args, far_args=0, scratch=()):
+def call(kernel, outs, args, far_args=0, scratch=(), aliases=None):
     return pl.pallas_call(
         kernel,
         out_shape=outs,
         in_specs=[FAR] * far_args + [VMEM] * (len(args) - far_args),
         out_specs=[VMEM] * len(outs),
         scratch_shapes=list(scratch),
+        input_output_aliases=aliases or {},
         compiler_params=pltpu.CompilerParams(vmem_limit_bytes=16 << 20),
     )(*args)
 
@@ -303,6 +351,8 @@
     field = near_out((rights, order), F32)
     face_outs = [far_out((len(faces), rights, tile), BF16) for faces, _, _ in groups]
     face_count = sum(len(faces) for faces, _, _ in groups)
+    listed = tiles.shape[2]
+    fetch = listed * FETCH // 16
     parts = total // count
     rows = code_rows(parts) + rights + held * parts
 
@@ -335,12 +385,14 @@
     for sweep in range(SWEEPS):
         if sweep == 0:
             got = near(lax.all_gather(packed, "sub", axis=0))
-            tile_block, matched, block, u, *faces = call(
+            matrix, fetched, matched, where, own, u, *faces = call(
                 functools.partial(opening_kernel, total),
                 [
-                    near_out(tiles.shape[2:], BF16),
+                    near_out((order, order), BF16),
+                    near_out((fetch, tile, tile), BF16),
                     near_out((matching.shape[2], 1, tile), I32),
-                    near_out((peers, 2 * count, count), BF16),
+                    near_out((total, peers * count), BF16),
+                    near_out((count, total), BF16),
                     field,
                     *face_outs,
                 ],
@@ -367,12 +419,23 @@
             arrived.append(near(swap(face, *how[1:4])))
         low_out = (near_out if sweep + 1 < SWEEPS else far_out)((rights, order), BF16)
         if sweep == 0:
-            base, low, tables, matrix = call(
-                functools.partial(local_first_kernel, groups),
-                [field, low_out, near_out((face_count, tile, tile), BF16), near_out((order, order), BF16)],
-                [far(tile_list[0, 0].T), u, rhs, tile_block, matched],
-                far_args=1,
-                scratch=[pltpu.SMEM(tile_list.shape[:1:-1], I32), pltpu.SemaphoreType.DMA],
+            base, low, tables, block, matrix = call(
+                functools.partial(local_first_kernel, groups, total),
+                [
+                    field,
+                    low_out,
+                    near_out((face_count, tile, tile), BF16),
+                    near_out((2 * count, peers * count), BF16),
+                    near_out((order, order), BF16),
+                ],
+                [far(tiles[0, 0]), far(tile_list[0, 0].T), u, rhs, matrix, fetched, matched, got, where, own],
+                far_args=2,
+                scratch=[
+                    pltpu.SMEM(tile_list.shape[:1:-1], I32),
+                    pltpu.VMEM((listed - fetch, tile, tile), BF16),
+                    pltpu.SemaphoreType.DMA((2,)),
+                ],
+                aliases={4: 4},
             )
         else:
             base, low = call(local_kernel, [field, low_out], [u, rhs, matrix])

time: 53.8 us -> 53.4 us (level)
  transfers between devices with their start and end apart: 12 -> 12, of which waited for: 3 -> 2; matrix products, arithmetic and copies ran while one was open for 0% -> 0% of each run, Pallas kernels for 8% -> 9%
where the time goes in v4:
time: 53.4 us; the launch traced here: 53.1 us
  blocking collectives  26.1 us (49%)
  starting transfers between devices  11.7 us (22%)
  Pallas kernels  9.98 us (19%)
  waiting for transfers between devices  4.61 us (9%)
  between operations  0.74 us (1%)
    all_to_all x2, blocking collectives, body(): lax.all_to_all(chunk, 'sub', split_axis=0, concat_axis=0, tiled=True)  14.6 us
    ppermute x12, starting transfers between devices, swap(): return lax.ppermute(shard, axis, pairs)  11.7 us
    all_gather x1, blocking collectives, body(): got = near(lax.all_gather(packed, 'sub', axis=0))  11.5 us
    pallas_call x10, Pallas kernels, call(): pl.pallas_call(kernel, out_shape=outs, in_specs=[FAR] * far_args + [VMEM]...  9.98 us
    ppermute x12, waiting for transfers between devices, swap(): return lax.ppermute(shard, axis, pairs)  4.61 us
  transfers between devices with their start and end apart: 12, of which 2 were waited for; matrix products, arithmetic and copies ran while one was open for 0% of the time, Pallas kernels for 9%

profile of v4, /device:TPU:0, one launch (start us, length us, event | category | flops | bytes accessed | tf_op | source)
XLA Modules:
  0.0 53.1 jit_solution(11220211387488315490)
XLA Ops:
  0.6 1.4 %shard_map.104 = (bf16[288,128]{1,0:T(8,128)(2,1)S(1)}, f32[16,1280]{1,0:T(8,128)S(1)}, bf16[1280,128]{1,0:T(8,128)(2,1)S(1)}, f32[1,1280]{1,0:T(1,128)S(1)}, s3...) custom-call(f32[16,1280]{1,0:T(8,128)} %bitcast.26, bf16[1280,128]{1,0:T(8,128)(2,1)} %bitcast.24, f32[64,512]{1,0:T(8,128)} %bitcast.25, ...), custom_call_target="tpu_custom_call" | custom-call | tf_op jit(solution)/shard_map/pallas_call | solution.py:292
  2.0 11.5 %all-gather = bf16[2304,128]{1,0:T(8,128)(2,1)S(1)} all-gather(bf16[288,128]{1,0:T(8,128)(2,1)S(1)} %get-tuple-element.40), channel_id=2, replica_groups=mesh['sub'=8,'reg'=4] {'sub'}, dimensions={0}, use_global_device_ids=true | all-gather | bytes 663552 | tf_op jit(solution)/shard_map/all_gather | solution.py:387
  13.5 1.5 %shard_map.105 = (bf16[1280,1280]{1,0:T(8,128)(2,1)S(1)}, bf16[50,128,128]{2,1,0:T(8,128)(2,1)S(1)}, s32[6,1,128]{2,1,0:T(1,128)S(1)}, bf16[512,1024]{1,0:T(8,12...) custom-call(bf16[80,128,128]{2,1,0:T(8,128)(2,1)} %bitcast.22, ...), custom_call_target="tpu_custom_call" | custom-call | tf_op jit(solution)/shard_map/pallas_call | solution.py:292
  14.9 3.7 %collective-permute-start.1 = (bf16[2,16,128]{2,1,0:T(8,128)(2,1)S(1)}, bf16[2,16,128]{2,1,0:T(8,128)(2,1)S(1)}, u32[]{:S(2)}, u32[]{:S(2)}) collective-permute-start(bf16[2,16,128]{2,1,0:T(8,128)(2,1)S(1)} %get-tuple-element.54), channel_id=1, source_target_pairs={{1,2},{2,1},{3,0},{0,3},{5,6},{6,5},{7,4},{4,7},{9,10},{10,9},{11,... | collective-permute-start | bytes 24584 | tf_op jit(solution)/shard_map/ppermute | solution.py:348
  18.6 1.1 %collective-permute-start = (bf16[1,16,128]{2,1,0:T(8,128)(2,1)S(1)}, bf16[1,16,128]{2,1,0:T(8,128)(2,1)S(1)}, u32[]{:S(2)}, u32[]{:S(2)}) collective-permute-start(bf16[1,16,128]{2,1,0:T(8,128)(2,1)S(1)} %get-tuple-element.53), channel_id=1, source_target_pairs={{4,8},{8,4},{12,16},{16,12},{20,24},{24,20},{28,0},{0,28},{5,9},{9... | collective-permute-start | bytes 12296 | tf_op jit(solution)/shard_map/ppermute | solution.py:348
  19.7 0.5 collective-permute-start.3
  20.2 2.6 %shard_map.106 = (f32[16,1280]{1,0:T(8,128)S(1)}, bf16[16,1280]{1,0:T(8,128)(2,1)}, bf16[6,128,128]{2,1,0:T(8,128)(2,1)S(1)}, bf16[256,1024]{1,0:T(8,128)(2,1)S(1)}, bf16[1280,1280]{1,0:T(8,128)(2,1)S(1)}) custom-call(bf16[80,128,128]{2,1,0:T(8,128)(2,1)} %bitcast.23, s32[2,80]{1,0:T(2,128)} %bitcast.30, ...), custom_call_target="tpu_custom_call", output_to_operand_aliasing={{4}: (4, {})} | custom-call | tf_op jit(solution)/shard_map/pallas_call | solution.py:292
  22.9 0.3 shard_map.107
  23.2 7.4 %all_to_all.10.got_ref = bf16[8,16,128]{2,1,0:T(8,128)(2,1)S(1)} all-to-all(bf16[8,16,128]{2,1,0:T(8,128)(2,1)S(1)} %get-tuple-element.57), channel_id=1, replica_groups=mesh['sub'=8,'reg'=4] {'sub'}, dimensions={0} | all-to-all | bytes 65536 | tf_op jit(solution)/shard_map/all_to_all | solution.py:413
  30.6 0.6 %shard_map.108 = (f32[16,1280]{1,0:T(8,128)S(1)}, bf16[1,16,128]{2,1,0:T(8,128)(2,1)S(1)}, bf16[2,16,128]{2,1,0:T(8,128)(2,1)S(1)}, bf16[2,16,128]{2,1,0:T(8,128)(2,1)S(1)}, bf16[1,16,128]{2,1,0:T(8,128)(2,1)S(1)}) custom-call(bf16[8,16,128]{2,1,0:T(8,128)(2,1)S(1)} %all_to_all.10.got_ref, bf16[256,1024]{1,0:T(8,128)(2,1)S(1)} %get-tuple-element.58.block_ref, ...), custom_call_target="tpu_custom_call" | custom-call | tf_op jit(solution)/shard_map/pallas_call | solution.py:292
  31.2 1.2 %collective-permute-start.5 = (bf16[2,16,128]{2,1,0:T(8,128)(2,1)S(1)}, bf16[2,16,128]{2,1,0:T(8,128)(2,1)S(1)}, u32[]{:S(2)}, u32[]{:S(2)}) collective-permute-start(bf16[2,16,128]{2,1,0:T(8,128)(2,1)S(1)} %get-tuple-element.64), channel_id=1, source_target_pairs={{1,2},{2,1},{3,0},{0,3},{5,6},{6,5},{7,4},{4,7},{9,10},{10,9},{11,... | collective-permute-start | bytes 24584 | tf_op jit(solution)/shard_map/ppermute | solution.py:348
  32.4 0.9 %collective-permute-start.6 = (bf16[2,16,128]{2,1,0:T(8,128)(2,1)S(1)}, bf16[2,16,128]{2,1,0:T(8,128)(2,1)S(1)}, u32[]{:S(2)}, u32[]{:S(2)}) collective-permute-start(bf16[2,16,128]{2,1,0:T(8,128)(2,1)S(1)} %get-tuple-element.65), channel_id=1, source_target_pairs={{0,1},{1,0},{2,3},{3,2},{4,5},{5,4},{6,7},{7,6},{8,9},{9,8},{10,11... | collective-permute-start | bytes 24584 | tf_op jit(solution)/shard_map/ppermute | solution.py:348
  33.4 0.7 %collective-permute-start.7 = (bf16[1,16,128]{2,1,0:T(8,128)(2,1)S(1)}, bf16[1,16,128]{2,1,0:T(8,128)(2,1)S(1)}, u32[]{:S(2)}, u32[]{:S(2)}) collective-permute-start(bf16[1,16,128]{2,1,0:T(8,128)(2,1)S(1)} %get-tuple-element.66), channel_id=1, source_target_pairs={{0,4},{4,0},{8,12},{12,8},{16,20},{20,16},{24,28},{28,24},{1,5},{5... | collective-permute-start | bytes 12296 | tf_op jit(solution)/shard_map/ppermute | solution.py:348
  34.0 1.0 %shard_map.109 = (f32[16,1280]{1,0:T(8,128)S(1)}, bf16[16,1280]{1,0:T(8,128)(2,1)}) custom-call(f32[16,1280]{1,0:T(8,128)S(1)} %get-tuple-element.60.u_ref, f32[16,1280]{1,0:T(8,128)S(1)} %get-tuple-element.43.r_ref.rhs_ref, bf16[1280,1280]{1,0:T(8,128)(2,1)S(1)} %get-tuple-element.61.matrix_ref), custom_call_target="tpu_custom_call" | custom-call | tf_op jit(solution)/shard_map/pallas_call | solution.py:292
  35.0 2.3 %collective-permute-done.4.refs_0_ = bf16[1,16,128]{2,1,0:T(8,128)(2,1)S(1)} collective-permute-done((bf16[1,16,128]{2,1,0:T(8,128)(2,1)S(1)}, bf16[1,16,128]{2,1,0:T(8,128)(2,1)S(1)}, u32[]{:S(2)}, u32[]{:S(2)}) %collective-permute-start.4) | collective-permute-done | bytes 4128 | tf_op jit(solution)/shard_map/ppermute | solution.py:348
  37.3 0.3 shard_map.110
  37.6 7.2 %all_to_all.11.got_ref = bf16[8,16,128]{2,1,0:T(8,128)(2,1)S(1)} all-to-all(bf16[8,16,128]{2,1,0:T(8,128)(2,1)S(1)} %get-tuple-element.67), channel_id=1, replica_groups=mesh['sub'=8,'reg'=4] {'sub'}, dimensions={0} | all-to-all | bytes 65536 | tf_op jit(solution)/shard_map/all_to_all | solution.py:413
  44.8 0.6 %shard_map.111 = (f32[16,1280]{1,0:T(8,128)S(1)}, bf16[1,16,128]{2,1,0:T(8,128)(2,1)S(1)}, bf16[2,16,128]{2,1,0:T(8,128)(2,1)S(1)}, bf16[2,16,128]{2,1,0:T(8,128)(2,1)S(1)}, bf16[1,16,128]{2,1,0:T(8,128)(2,1)S(1)}) custom-call(bf16[8,16,128]{2,1,0:T(8,128)(2,1)S(1)} %all_to_all.11.got_ref, bf16[256,1024]{1,0:T(8,128)(2,1)S(1)} %get-tuple-element.58.block_ref, ...), custom_call_target="tpu_custom_call" | custom-call | tf_op jit(solution)/shard_map/pallas_call | solution.py:292
  45.4 2.9 %collective-permute-start.9 = (bf16[2,16,128]{2,1,0:T(8,128)(2,1)S(1)}, bf16[2,16,128]{2,1,0:T(8,128)(2,1)S(1)}, u32[]{:S(2)}, u32[]{:S(2)}) collective-permute-start(bf16[2,16,128]{2,1,0:T(8,128)(2,1)S(1)} %get-tuple-element.73), channel_id=1, source_target_pairs={{1,2},{2,1},{3,0},{0,3},{5,6},{6,5},{7,4},{4,7},{9,10},{10,9},{11,... | collective-permute-start | bytes 24584 | tf_op jit(solution)/shard_map/ppermute | solution.py:348
  48.4 0.0 collective-permute-start.10
  48.4 0.7 %collective-permute-start.11 = (bf16[1,16,128]{2,1,0:T(8,128)(2,1)S(1)}, bf16[1,16,128]{2,1,0:T(8,128)(2,1)S(1)}, u32[]{:S(2)}, u32[]{:S(2)}) collective-permute-start(bf16[1,16,128]{2,1,0:T(8,128)(2,1)S(1)} %get-tuple-element.75), channel_id=1, source_target_pairs={{0,4},{4,0},{8,12},{12,8},{16,20},{20,16},{24,28},{28,24},{1,5},{5... | collective-permute-start | bytes 12296 | tf_op jit(solution)/shard_map/ppermute | solution.py:348
  49.0 1.0 %shard_map.112 = (f32[16,1280]{1,0:T(8,128)S(1)}, bf16[16,1280]{1,0:T(8,128)(2,1)}) custom-call(f32[16,1280]{1,0:T(8,128)S(1)} %get-tuple-element.69.u_ref, f32[16,1280]{1,0:T(8,128)S(1)} %get-tuple-element.43.r_ref.rhs_ref, bf16[1280,1280]{1,0:T(8,128)(2,1)S(1)} %get-tuple-element.61.matrix_ref), custom_call_target="tpu_custom_call" | custom-call | tf_op jit(solution)/shard_map/pallas_call | solution.py:292
  50.0 2.3 %collective-permute-done.8.refs_0_ = bf16[1,16,128]{2,1,0:T(8,128)(2,1)S(1)} collective-permute-done((bf16[1,16,128]{2,1,0:T(8,128)(2,1)S(1)}, bf16[1,16,128]{2,1,0:T(8,128)(2,1)S(1)}, u32[]{:S(2)}, u32[]{:S(2)}) %collective-permute-start.8) | collective-permute-done | bytes 4128 | tf_op jit(solution)/shard_map/ppermute | solution.py:348
  52.3 0.8 %shard_map.113 = bf16[16,1280]{1,0:T(8,128)(2,1)} custom-call(bf16[6,128,128]{2,1,0:T(8,128)(2,1)S(1)} %get-tuple-element.51.tables_ref, f32[6,16,128]{2,1,0:T(8,128)S(1)} %get-tuple-element.44.masks_ref, f32[16,1280]{1,0:T(8,128)S(1)} %get-tuple-element.71.base_ref, bf16[1,16,128]{2,1,0:T(8,128)(2,1)S(1)} %collective-permute-done.8.refs_0_, ...), custom_call_target="tpu_custom_call" | custom-call | tf_op jit(solution)/shard_map/pallas_call | solution.py:292
  (13 shorter events, 0.0 us)
Async XLA Ops:
  14.9 8.0 %collective-permute-start.1 = (bf16[2,16,128]{2,1,0:T(8,128)(2,1)S(1)}, bf16[2,16,128]{2,1,0:T(8,128)(2,1)S(1)}, u32[]{:S(2)}, u32[]{:S(2)}) collective-permute-start(bf16[2,16,128]{2,1,0:T(8,128)(2,1)S(1)} %get-tuple-element.54), channel_id=1, source_target_pairs={{1,2},{2,1},{3,0},{0,3},{5,6},{6,5},{7,4},{4,7},{9,10},{10,9},{11,... | collective-permute-start | bytes 24584 | tf_op jit(solution)/shard_map/ppermute | solution.py:348
  18.6 4.3 %collective-permute-start.2 = (bf16[2,16,128]{2,1,0:T(8,128)(2,1)S(1)}, bf16[2,16,128]{2,1,0:T(8,128)(2,1)S(1)}, u32[]{:S(2)}, u32[]{:S(2)}) collective-permute-start(bf16[2,16,128]{2,1,0:T(8,128)(2,1)S(1)} %get-tuple-element.55), channel_id=1, source_target_pairs={{0,1},{1,0},{2,3},{3,2},{4,5},{5,4},{6,7},{7,6},{8,9},{9,8},{10,11... | collective-permute-start | bytes 24584 | tf_op jit(solution)/shard_map/ppermute | solution.py:348
  18.6 4.3 %collective-permute-start = (bf16[1,16,128]{2,1,0:T(8,128)(2,1)S(1)}, bf16[1,16,128]{2,1,0:T(8,128)(2,1)S(1)}, u32[]{:S(2)}, u32[]{:S(2)}) collective-permute-start(bf16[1,16,128]{2,1,0:T(8,128)(2,1)S(1)} %get-tuple-element.53), channel_id=1, source_target_pairs={{4,8},{8,4},{12,16},{16,12},{20,24},{24,20},{28,0},{0,28},{5,9},{9... | collective-permute-start | bytes 12296 | tf_op jit(solution)/shard_map/ppermute | solution.py:348
  19.7 3.1 %collective-permute-start.3 = (bf16[1,16,128]{2,1,0:T(8,128)(2,1)S(1)}, bf16[1,16,128]{2,1,0:T(8,128)(2,1)S(1)}, u32[]{:S(2)}, u32[]{:S(2)}) collective-permute-start(bf16[1,16,128]{2,1,0:T(8,128)(2,1)S(1)} %get-tuple-element.56), channel_id=1, source_target_pairs={{0,4},{4,0},{8,12},{12,8},{16,20},{20,16},{24,28},{28,24},{1,5},{5... | collective-permute-start | bytes 12296 | tf_op jit(solution)/shard_map/ppermute | solution.py:348
  31.2 6.1 %collective-permute-start.5 = (bf16[2,16,128]{2,1,0:T(8,128)(2,1)S(1)}, bf16[2,16,128]{2,1,0:T(8,128)(2,1)S(1)}, u32[]{:S(2)}, u32[]{:S(2)}) collective-permute-start(bf16[2,16,128]{2,1,0:T(8,128)(2,1)S(1)} %get-tuple-element.64), channel_id=1, source_target_pairs={{1,2},{2,1},{3,0},{0,3},{5,6},{6,5},{7,4},{4,7},{9,10},{10,9},{11,... | collective-permute-start | bytes 24584 | tf_op jit(solution)/shard_map/ppermute | solution.py:348
  32.4 4.9 %collective-permute-start.6 = (bf16[2,16,128]{2,1,0:T(8,128)(2,1)S(1)}, bf16[2,16,128]{2,1,0:T(8,128)(2,1)S(1)}, u32[]{:S(2)}, u32[]{:S(2)}) collective-permute-start(bf16[2,16,128]{2,1,0:T(8,128)(2,1)S(1)} %get-tuple-element.65), channel_id=1, source_target_pairs={{0,1},{1,0},{2,3},{3,2},{4,5},{5,4},{6,7},{7,6},{8,9},{9,8},{10,11... | collective-permute-start | bytes 24584 | tf_op jit(solution)/shard_map/ppermute | solution.py:348
  33.4 3.9 %collective-permute-start.4 = (bf16[1,16,128]{2,1,0:T(8,128)(2,1)S(1)}, bf16[1,16,128]{2,1,0:T(8,128)(2,1)S(1)}, u32[]{:S(2)}, u32[]{:S(2)}) collective-permute-start(bf16[1,16,128]{2,1,0:T(8,128)(2,1)S(1)} %get-tuple-element.63), channel_id=1, source_target_pairs={{4,8},{8,4},{12,16},{16,12},{20,24},{24,20},{28,0},{0,28},{5,9},{9... | collective-permute-start | bytes 12296 | tf_op jit(solution)/shard_map/ppermute | solution.py:348
  33.4 3.9 %collective-permute-start.7 = (bf16[1,16,128]{2,1,0:T(8,128)(2,1)S(1)}, bf16[1,16,128]{2,1,0:T(8,128)(2,1)S(1)}, u32[]{:S(2)}, u32[]{:S(2)}) collective-permute-start(bf16[1,16,128]{2,1,0:T(8,128)(2,1)S(1)} %get-tuple-element.66), channel_id=1, source_target_pairs={{0,4},{4,0},{8,12},{12,8},{16,20},{20,16},{24,28},{28,24},{1,5},{5... | collective-permute-start | bytes 12296 | tf_op jit(solution)/shard_map/ppermute | solution.py:348
  45.4 6.9 %collective-permute-start.9 = (bf16[2,16,128]{2,1,0:T(8,128)(2,1)S(1)}, bf16[2,16,128]{2,1,0:T(8,128)(2,1)S(1)}, u32[]{:S(2)}, u32[]{:S(2)}) collective-permute-start(bf16[2,16,128]{2,1,0:T(8,128)(2,1)S(1)} %get-tuple-element.73), channel_id=1, source_target_pairs={{1,2},{2,1},{3,0},{0,3},{5,6},{6,5},{7,4},{4,7},{9,10},{10,9},{11,... | collective-permute-start | bytes 24584 | tf_op jit(solution)/shard_map/ppermute | solution.py:348
  48.4 3.9 %collective-permute-start.10 = (bf16[2,16,128]{2,1,0:T(8,128)(2,1)S(1)}, bf16[2,16,128]{2,1,0:T(8,128)(2,1)S(1)}, u32[]{:S(2)}, u32[]{:S(2)}) collective-permute-start(bf16[2,16,128]{2,1,0:T(8,128)(2,1)S(1)} %get-tuple-element.74), channel_id=1, source_target_pairs={{0,1},{1,0},{2,3},{3,2},{4,5},{5,4},{6,7},{7,6},{8,9},{9,8},{10,11... | collective-permute-start | bytes 24584 | tf_op jit(solution)/shard_map/ppermute | solution.py:348
  48.4 3.9 %collective-permute-start.8 = (bf16[1,16,128]{2,1,0:T(8,128)(2,1)S(1)}, bf16[1,16,128]{2,1,0:T(8,128)(2,1)S(1)}, u32[]{:S(2)}, u32[]{:S(2)}) collective-permute-start(bf16[1,16,128]{2,1,0:T(8,128)(2,1)S(1)} %get-tuple-element.72), channel_id=1, source_target_pairs={{4,8},{8,4},{12,16},{16,12},{20,24},{24,20},{28,0},{0,28},{5,9},{9... | collective-permute-start | bytes 12296 | tf_op jit(solution)/shard_map/ppermute | solution.py:348
  48.4 3.9 %collective-permute-start.11 = (bf16[1,16,128]{2,1,0:T(8,128)(2,1)S(1)}, bf16[1,16,128]{2,1,0:T(8,128)(2,1)S(1)}, u32[]{:S(2)}, u32[]{:S(2)}) collective-permute-start(bf16[1,16,128]{2,1,0:T(8,128)(2,1)S(1)} %get-tuple-element.75), channel_id=1, source_target_pairs={{0,4},{4,0},{8,12},{12,8},{16,20},{20,16},{24,28},{28,24},{1,5},{5... | collective-permute-start | bytes 12296 | tf_op jit(solution)/shard_map/ppermute | solution.py:348
